TPU v7x, 32 devices: a whole 2x2x4 slice. The times are simulated.
32 devices in a mesh: fsdp: 2 (over x), ctx: 4 (over y, core), tp: 4 (over z).
Axes of the slice: x: 2, y: 2, z: 4, core: 2. Of those that a mesh axis runs over, the one named last changes fastest.
Arguments:
- block_in: bfloat16 [8, 1024, 2048], P('fsdp', 'ctx', 'tp'), may hold values from -6 to 6
- seg_ids: int32 [8, 1024], P('fsdp'), may hold values from 0 to 7, never falling along the last dimension, each value on 1 to 512 neighbouring positions
- out_cot: bfloat16 [8, 1024, 2048], P('fsdp', 'ctx'), may hold values from -6 to 6
- norm_gain: bfloat16 [2048], P('tp'), may hold values from 0.099609375 to 1.8984375
- mid_gain: bfloat16 [2048], P('tp'), may hold values from 0.099609375 to 1.8984375
- gelu_proj: bfloat16 [2048, 2816], P(('fsdp', 'ctx'), 'tp'), may hold values from -0.125 to 0.125
- scan_proj: bfloat16 [2048, 2816], P(('fsdp', 'ctx'), 'tp'), may hold values from -0.125 to 0.125
- out_proj: bfloat16 [2816, 2048], P('tp', ('fsdp', 'ctx')), may hold values from -0.4375 to 0.4375
- gate_proj: bfloat16 [2048, 6144], P(('fsdp', 'ctx'), 'tp'), may hold values from -0.125 to 0.125
- up_proj: bfloat16 [2048, 6144], P(('fsdp', 'ctx'), 'tp'), may hold values from -0.125 to 0.125
- down_proj: bfloat16 [6144, 2048], P('tp', ('fsdp', 'ctx')), may hold values from -0.109375 to 0.109375
- conv_kernel: float32 [4, 2816], P(None, 'tp'), may hold values from -3 to 3
- conv_bias: float32 [2816], P('tp'), may hold values from -3 to 3
- rate_gate: bfloat16 [16, 176, 176], P('tp'), may hold values from -0.4375 to 0.4375
- input_gate: bfloat16 [16, 176, 176], P('tp'), may hold values from -0.4375 to 0.4375
- rate_bias: float32 [2816], P('tp'), may hold values from -4 to 4
- input_bias: float32 [2816], P('tp'), may hold values from -4 to 4
- decay_param: float32 [2816], P('tp'), may hold values from -16 to -4
Outputs:
- block_out: bfloat16 [8, 1024, 2048], P('fsdp', 'ctx', 'tp')
- grad_in: float32 [8, 1024, 2048], P('fsdp', 'ctx', 'tp')
- grad_norm_gain: float32 [2048], P('tp')
- grad_mid_gain: float32 [2048], P('tp')
- grad_gelu_proj: float32 [2048, 2816], P(('fsdp', 'ctx'), 'tp')
- grad_scan_proj: float32 [2048, 2816], P(('fsdp', 'ctx'), 'tp')
- grad_out_proj: float32 [2816, 2048], P('tp', ('fsdp', 'ctx'))
- grad_gate_proj: float32 [2048, 6144], P(('fsdp', 'ctx'), 'tp')
- grad_up_proj: float32 [2048, 6144], P(('fsdp', 'ctx'), 'tp')
- grad_down_proj: float32 [6144, 2048], P('tp', ('fsdp', 'ctx'))
- grad_conv_kernel: float32 [4, 2816], P(None, 'tp')
- grad_conv_bias: float32 [2816], P('tp')
- grad_rate_gate: float32 [16, 176, 176], P('tp')
- grad_input_gate: float32 [16, 176, 176], P('tp')
- grad_rate_bias: float32 [2816], P('tp')
- grad_input_bias: float32 [2816], P('tp')
- grad_decay_param: float32 [2816], P('tp')
Inputs may be any that keep to these rules, and one draw needn't show every extreme that they name: `seg_ids`: in every row the document numbers never fall; each of the 8 documents covers 1 to 512 positions, and one covers exactly 512.
All inputs are finite; a program needn't handle non-finite values.
Results may differ from a plain program's by a relative error of at most 0.0095.
Values may be sent and summed in bfloat16 or wider, within the bound.
A program may use at most 320 MiB of HBM per device.

v0:
```python
import jax
import jax.numpy as jnp
from jax import lax
from jax.sharding import PartitionSpec as P

CONV = 4


eps_norm = 1e-06


def from_behind(value, axis, steps):
    count = lax.axis_size(axis)
    leading, last = (max(0, -steps), min(count, count - steps))
    return lax.ppermute(value, axis, [(source, source + steps) for source in range(leading, last)])


def entering(value, axis, join, neutral, backward):
    count, mine = (lax.axis_size(axis), lax.axis_index(axis))
    pieces = jax.tree.map(lambda part: lax.all_gather(part, axis), value)
    if backward:
        pieces = jax.tree.map(lambda part: part[::-1], pieces)
        mine = count - 1 - mine
    total = jax.tree.map(
        lambda part, zero: jnp.full_like(part, 0) + jnp.asarray(zero, part.dtype), value, neutral
    )

    def step(position, total):
        longer = join(total, jax.tree.map(lambda part: part[position], pieces))
        return jax.tree.map(lambda new, old: jnp.where(position < mine, new, old), longer, total)

    return lax.fori_loop(0, count - 1, step, total)


def rms_scale(values, gain_vec):
    return (
        values * lax.rsqrt(jnp.mean(values * values, axis=-1, keepdims=True) + eps_norm) * gain_vec
    )


def gelu_tanh(values):
    return jax.nn.gelu(values, approximate=True)


def gate_values(pre_rate, pre_input, decay_param):
    rate_vals = jax.nn.sigmoid(pre_rate)
    input_vals = jax.nn.sigmoid(pre_input)
    log_a = -8.0 * jax.nn.softplus(decay_param) * rate_vals
    return (jnp.exp(log_a), jnp.sqrt(-jnp.expm1(2.0 * log_a)) * input_vals)


def combine(first_part, second_part):
    return (first_part[0] * second_part[0], second_part[0] * first_part[1] + second_part[1])


def matmul(left, right):
    return jnp.dot(left, right, preferred_element_type=jnp.float32)


def matmul_rt(left, right):
    return lax.dot_general(
        left, right, (((1,), (1,)), ((), ())), preferred_element_type=jnp.float32
    )


def matmul_lt(left, right):
    return lax.dot_general(
        left, right, (((0,), (0,)), ((), ())), preferred_element_type=jnp.float32
    )


def shards(
    block_in,
    seg_ids,
    out_cot,
    norm_gain,
    mid_gain,
    gelu_proj,
    scan_proj,
    out_proj,
    gate_proj,
    up_proj,
    down_proj,
    conv_kernel,
    conv_bias,
    rate_gate,
    input_gate,
    rate_bias,
    input_bias,
    decay_param,
):
    seq_count, tok_count, part_width = block_in.shape
    row_count = seq_count * tok_count
    full_in, gain_one, gain_two = (
        lax.all_gather(block_in, "tp", axis=2, tiled=True),
        lax.all_gather(norm_gain, "tp", axis=0, tiled=True),
        lax.all_gather(mid_gain, "tp", axis=0, tiled=True),
    )
    w_gelu, w_scan, w_out, w_gate, w_up, w_down = (
        lax.all_gather(gelu_proj, ("fsdp", "ctx"), axis=0, tiled=True),
        lax.all_gather(scan_proj, ("fsdp", "ctx"), axis=0, tiled=True),
        lax.all_gather(out_proj, ("fsdp", "ctx"), axis=1, tiled=True),
        lax.all_gather(gate_proj, ("fsdp", "ctx"), axis=0, tiled=True),
        lax.all_gather(up_proj, ("fsdp", "ctx"), axis=0, tiled=True),
        lax.all_gather(down_proj, ("fsdp", "ctx"), axis=1, tiled=True),
    )
    full_width = full_in.shape[2]
    rec_width = w_gelu.shape[1]
    head_count = rate_gate.shape[0]
    head_size = rate_gate.shape[1]
    x_rows = full_in.reshape(row_count, full_width).astype(jnp.float32)
    normed_f, norm_one_back = jax.vjp(rms_scale, x_rows, gain_one.astype(jnp.float32))
    normed = normed_f.astype(jnp.bfloat16)
    y_pre = matmul(normed, w_gelu)
    y_act, y_back = jax.vjp(gelu_tanh, y_pre)
    x_branch = matmul(normed, w_scan).astype(jnp.bfloat16).reshape(seq_count, tok_count, rec_width)
    margin_len = CONV - 1
    start_tok = lax.axis_index("ctx") * tok_count
    padded_ids = jnp.concatenate(
        [
            jnp.full((seq_count, margin_len), -1, jnp.int32),
            seg_ids,
            jnp.full((seq_count, margin_len), -2, jnp.int32),
        ],
        axis=1,
    )
    window_ids = lax.dynamic_slice_in_dim(padded_ids, start_tok, tok_count + 2 * margin_len, 1)
    own_ids = window_ids[:, margin_len : margin_len + tok_count]
    back_masks = [
        (window_ids[:, margin_len - offset : margin_len - offset + tok_count] == own_ids).astype(
            jnp.float32
        )[..., None]
        for offset in range(CONV)
    ]
    ahead_masks = [
        (window_ids[:, margin_len + offset : margin_len + offset + tok_count] == own_ids).astype(
            jnp.float32
        )[..., None]
        for offset in range(CONV)
    ]
    prev_edge = from_behind(x_branch[:, tok_count - margin_len :, :], "ctx", 1)
    ext_x = jnp.concatenate([prev_edge, x_branch], axis=1)
    conv_sum = conv_bias + jnp.zeros((seq_count, tok_count, rec_width), jnp.float32)
    for offset in range(CONV):
        conv_sum = (
            conv_sum
            + conv_kernel[offset]
            * ext_x[:, margin_len - offset : margin_len - offset + tok_count].astype(jnp.float32)
            * back_masks[offset]
        )
    conv_out = conv_sum.astype(jnp.bfloat16)
    conv_vals = conv_out.astype(jnp.float32)
    heads_in = conv_out.reshape(row_count, head_count, head_size)
    pre_rate = (
        jnp.einsum("rhi,hij->rhj", heads_in, rate_gate, preferred_element_type=jnp.float32).reshape(
            row_count, rec_width
        )
        + rate_bias
    )
    pre_input = (
        jnp.einsum(
            "rhi,hij->rhj", heads_in, input_gate, preferred_element_type=jnp.float32
        ).reshape(row_count, rec_width)
        + input_bias
    )
    (decays, in_scale), gate_back = jax.vjp(gate_values, pre_rate, pre_input, decay_param)
    in_scale3 = in_scale.reshape(seq_count, tok_count, rec_width)
    coeffs = decays.reshape(seq_count, tok_count, rec_width) * back_masks[1]
    inputs = in_scale3 * conv_vals
    cum_coef, local_state = lax.associative_scan(combine, (coeffs, inputs), axis=1)
    ones_row = jnp.ones((seq_count, rec_width), jnp.float32)
    zeros_row = jnp.zeros((seq_count, rec_width), jnp.float32)
    _, state_in = entering(
        (cum_coef[:, -1], local_state[:, -1]), "ctx", combine, (ones_row, zeros_row), False
    )
    states = local_state + cum_coef * state_in[:, None, :]
    state_rows = states.reshape(row_count, rec_width)
    mixed_in = (state_rows * y_act).astype(jnp.bfloat16)
    rec_part = matmul(mixed_in, w_out)
    col_start = lax.axis_index("tp") * part_width
    rec_total = lax.psum(rec_part, "tp")
    mid_rows = x_rows + rec_total
    normed_mid_f, norm_two_back = jax.vjp(rms_scale, mid_rows, gain_two.astype(jnp.float32))
    normed_mid = normed_mid_f.astype(jnp.bfloat16)
    gate_pre = matmul(normed_mid, w_gate)
    up_pre = matmul(normed_mid, w_up)
    gate_act, gate_act_back = jax.vjp(gelu_tanh, gate_pre)
    hidden = (gate_act * up_pre).astype(jnp.bfloat16)
    mlp_slice = lax.psum_scatter(matmul(hidden, w_down), "tp", scatter_dimension=1, tiled=True)
    mid_own = lax.dynamic_slice_in_dim(mid_rows, col_start, part_width, 1)
    block_out = (mid_own + mlp_slice).astype(jnp.bfloat16).reshape(seq_count, tok_count, part_width)
    cot_rows = out_cot.reshape(row_count, full_width)
    hid_grad = matmul_rt(cot_rows, w_down)
    grad_down = matmul_lt(hidden, cot_rows)
    gate_grad = gate_act_back(hid_grad * up_pre)[0].astype(jnp.bfloat16)
    up_grad = (hid_grad * gate_act).astype(jnp.bfloat16)
    grad_gate = matmul_lt(normed_mid, gate_grad)
    grad_up = matmul_lt(normed_mid, up_grad)
    mid_part = matmul_rt(gate_grad, w_gate) + matmul_rt(up_grad, w_up)
    mid_norm_grad = lax.psum(mid_part, "tp")
    mid_from_norm, gain_two_grad = norm_two_back(mid_norm_grad)
    mid_grad = cot_rows.astype(jnp.float32) + mid_from_norm
    rec_grad = mid_grad.astype(jnp.bfloat16)
    mixed_grad = matmul_rt(rec_grad, w_out)
    grad_out = matmul_lt(mixed_in, rec_grad)
    state_direct = (mixed_grad * y_act).reshape(seq_count, tok_count, rec_width)
    y_grad = y_back(mixed_grad * state_rows)[0].astype(jnp.bfloat16)
    grad_gelu = matmul_lt(normed, y_grad)
    in_part = matmul_rt(y_grad, w_gelu)
    next_coef = jnp.concatenate(
        [coeffs[:, 1:], jnp.ones((seq_count, 1, rec_width), jnp.float32)], axis=1
    )
    tail_coef, local_grad = lax.associative_scan(
        combine, (next_coef, state_direct), reverse=True, axis=1
    )
    head_coef = coeffs[:, 0]
    _, grad_in_state = entering(
        (head_coef * tail_coef[:, 0], head_coef * local_grad[:, 0]),
        "ctx",
        combine,
        (ones_row, zeros_row),
        True,
    )
    state_grad = local_grad + tail_coef * grad_in_state[:, None, :]
    prev_states = jnp.concatenate([state_in[:, None, :], states[:, :-1]], axis=1)
    decay_grad = (state_grad * prev_states * back_masks[1]).reshape(row_count, rec_width)
    scale_grad = (state_grad * conv_vals).reshape(row_count, rec_width)
    conv_direct = (state_grad * in_scale3).reshape(row_count, rec_width)
    rate_raw, input_raw, grad_decay = gate_back((decay_grad, scale_grad))
    rate_grad = rate_raw.astype(jnp.bfloat16)
    input_grad = input_raw.astype(jnp.bfloat16)
    rate_heads = rate_grad.reshape(row_count, head_count, head_size)
    input_heads = input_grad.reshape(row_count, head_count, head_size)
    grad_rate_gate = jnp.einsum(
        "rhi,rhj->hij", heads_in, rate_heads, preferred_element_type=jnp.float32
    )
    grad_input_gate = jnp.einsum(
        "rhi,rhj->hij", heads_in, input_heads, preferred_element_type=jnp.float32
    )
    grad_rate_bias = jnp.sum(rate_grad.astype(jnp.float32), axis=0)
    grad_input_bias = jnp.sum(input_grad.astype(jnp.float32), axis=0)
    gate_back_in = jnp.einsum(
        "rhj,hij->rhi", rate_heads, rate_gate, preferred_element_type=jnp.float32
    ) + jnp.einsum("rhj,hij->rhi", input_heads, input_gate, preferred_element_type=jnp.float32)
    conv_grad = (
        (conv_direct + gate_back_in.reshape(row_count, rec_width))
        .astype(jnp.bfloat16)
        .reshape(seq_count, tok_count, rec_width)
    )
    next_edge = from_behind(conv_grad[:, :margin_len, :], "ctx", -1)
    ext_grad = jnp.concatenate([conv_grad, next_edge], axis=1)
    conv_grad_f = conv_grad.astype(jnp.float32)
    branch_grad = jnp.zeros((seq_count, tok_count, rec_width), jnp.float32)
    kernel_rows = []
    for offset in range(CONV):
        branch_grad = (
            branch_grad
            + conv_kernel[offset]
            * ext_grad[:, offset : offset + tok_count].astype(jnp.float32)
            * ahead_masks[offset]
        )
        kernel_rows.append(
            jnp.sum(
                conv_grad_f
                * ext_x[:, margin_len - offset : margin_len - offset + tok_count].astype(
                    jnp.float32
                )
                * back_masks[offset],
                axis=(0, 1),
            )
        )
    grad_kernel = jnp.stack(kernel_rows)
    grad_conv = jnp.sum(conv_grad_f, axis=(0, 1))
    branch_low = branch_grad.astype(jnp.bfloat16).reshape(row_count, rec_width)
    grad_scan = matmul_lt(normed, branch_low)
    in_part = in_part + matmul_rt(branch_low, w_scan)
    in_from_norm, gain_one_part = norm_one_back(in_part)
    in_slice, gain_one_slice = (
        lax.psum_scatter(in_from_norm, "tp", scatter_dimension=1, tiled=True),
        lax.psum_scatter(gain_one_part, "tp", scatter_dimension=0, tiled=True),
    )
    grad_in = (lax.dynamic_slice_in_dim(mid_grad, col_start, part_width, 1) + in_slice).reshape(
        seq_count, tok_count, part_width
    )
    gain_two_slice = lax.dynamic_slice_in_dim(gain_two_grad, col_start, part_width, 0)
    grad_gelu_s, grad_scan_s, grad_out_s, grad_gate_s, grad_up_s, grad_down_s = (
        lax.psum_scatter(grad_gelu, ("fsdp", "ctx"), scatter_dimension=0, tiled=True),
        lax.psum_scatter(grad_scan, ("fsdp", "ctx"), scatter_dimension=0, tiled=True),
        lax.psum_scatter(grad_out, ("fsdp", "ctx"), scatter_dimension=1, tiled=True),
        lax.psum_scatter(grad_gate, ("fsdp", "ctx"), scatter_dimension=0, tiled=True),
        lax.psum_scatter(grad_up, ("fsdp", "ctx"), scatter_dimension=0, tiled=True),
        lax.psum_scatter(grad_down, ("fsdp", "ctx"), scatter_dimension=1, tiled=True),
    )
    (
        gain_one_total,
        gain_two_total,
        kernel_total,
        conv_total,
        rate_gate_total,
        input_gate_total,
        rate_bias_total,
        input_bias_total,
        decay_total,
    ) = lax.psum(
        (
            gain_one_slice,
            gain_two_slice,
            grad_kernel,
            grad_conv,
            grad_rate_gate,
            grad_input_gate,
            grad_rate_bias,
            grad_input_bias,
            grad_decay,
        ),
        ("fsdp", "ctx"),
    )
    return (
        block_out,
        grad_in,
        gain_one_total,
        gain_two_total,
        grad_gelu_s,
        grad_scan_s,
        grad_out_s,
        grad_gate_s,
        grad_up_s,
        grad_down_s,
        kernel_total,
        conv_total,
        rate_gate_total,
        input_gate_total,
        rate_bias_total,
        input_bias_total,
        decay_total,
    )


def solution(mesh):
    in_specs = (
        P("fsdp", "ctx", "tp"),
        P("fsdp", None),
        P("fsdp", "ctx", None),
        P("tp"),
        P("tp"),
        P(("fsdp", "ctx"), "tp"),
        P(("fsdp", "ctx"), "tp"),
        P("tp", ("fsdp", "ctx")),
        P(("fsdp", "ctx"), "tp"),
        P(("fsdp", "ctx"), "tp"),
        P("tp", ("fsdp", "ctx")),
        P(None, "tp"),
        P("tp"),
        P("tp", None, None),
        P("tp", None, None),
        P("tp"),
        P("tp"),
        P("tp"),
    )
    out_specs = (
        P("fsdp", "ctx", "tp"),
        P("fsdp", "ctx", "tp"),
        P("tp"),
        P("tp"),
        P(("fsdp", "ctx"), "tp"),
        P(("fsdp", "ctx"), "tp"),
        P("tp", ("fsdp", "ctx")),
        P(("fsdp", "ctx"), "tp"),
        P(("fsdp", "ctx"), "tp"),
        P("tp", ("fsdp", "ctx")),
        P(None, "tp"),
        P("tp"),
        P("tp", None, None),
        P("tp", None, None),
        P("tp"),
        P("tp"),
        P("tp"),
    )
    return jax.shard_map(shards, mesh=mesh, in_specs=in_specs, out_specs=out_specs, check_vma=False)
```

profile of v0, /device:TPU:10, one launch (start us, length us, event | category | flops | bytes accessed | tf_op | source)
XLA Modules:
  0.0 2522.3 jit_solution(14394685174451569282)
XLA Ops:
  10.7 12.1 all-gather.4
  25.3 63.8 %all-gather.14.cloned.1.call-done = bf16[4,256,2048]{2,1,0:T(8,128)(2,1)} async-done(((bf16[4,256,512]{2,1,0:T(8,128)(2,1)}), bf16[4,256,2048]{2,1,0:T(8,128)(2,1)}) %all-gather.14.cloned.1.call-update) | async-done | bytes 4194320 | tf_op jit(solution)/shard_map/all_gather | solution.py:95
  96.1 27.6 %all-gather.16.cloned.1.call-done = bf16[2048,704]{0,1:T(8,128)(2,1)} async-done(((bf16[256,704]{0,1:T(8,128)(2,1)}), bf16[2048,704]{0,1:T(8,128)(2,1)}) %all-gather.16.cloned.1.call-update) | async-done | bytes 2883600 | tf_op jit(solution)/shard_map/all_gather | solution.py:101
  546.4 12.1 all-gather.5
  558.5 275.5 %all-reduce.73.cloned.1.call-done = f32[1024,2048]{1,0:T(8,128)} async-done(((f32[1024,2048]{1,0:T(8,128)}), f32[1024,2048]{1,0:T(8,128)}) %all-reduce.73.cloned.1.call-update) | async-done | bytes 8388624 | tf_op jit(solution)/shard_map/psum | solution.py:181
  845.9 36.3 %all-gather.22.cloned.1.call-done = bf16[2048,1536]{1,0:T(8,128)(2,1)} async-done(((bf16[256,1536]{1,0:T(8,128)(2,1)}), bf16[2048,1536]{1,0:T(8,128)(2,1)}) %all-gather.22.cloned.1.call-update) | async-done | bytes 6291472 | tf_op jit(solution)/shard_map/all_gather | solution.py:103
  894.1 35.6 %all-gather.24.cloned.1.call-done = bf16[2048,1536]{1,0:T(8,128)(2,1)} async-done(((bf16[256,1536]{1,0:T(8,128)(2,1)}), bf16[2048,1536]{1,0:T(8,128)(2,1)}) %all-gather.24.cloned.1.call-update) | async-done | bytes 6291472 | tf_op jit(solution)/shard_map/all_gather | solution.py:104
  929.7 11.9 fusion.118
  941.6 36.7 %all-gather.26.cloned.1.call-done = bf16[1536,2048]{1,0:T(8,128)(2,1)} async-done(((bf16[1536,256]{1,0:T(8,128)(2,1)}), bf16[1536,2048]{1,0:T(8,128)(2,1)}) %all-gather.26.cloned.1.call-update) | async-done | bytes 6291472 | tf_op jit(solution)/shard_map/all_gather | solution.py:105
  978.3 18.6 multiply_convert_fusion.1
  1051.5 12.8 slice.658
  1064.3 12.7 slice.665
  1077.1 12.8 slice.656
  1101.7 205.1 %all-reduce.75.cloned.1.call-done = f32[1024,2048]{1,0:T(8,128)} async-done(((f32[1024,2048]{1,0:T(8,128)}), f32[1024,2048]{1,0:T(8,128)}) %all-reduce.75.cloned.1.call-update) | async-done | bytes 8388624 | tf_op jit(solution)/shard_map/psum | solution.py:200
  1355.9 12.7 slice.660
  1368.6 12.8 slice.662
  1637.5 12.8 slice.718
  1691.7 24.7 rev.15
  1716.5 24.8 rev.14
  1854.2 12.5 fusion.122
  1867.0 12.5 fusion.123
  1879.5 12.2 fusion.124
  1894.6 12.7 all-reduce.66
  1907.4 24.0 all-reduce.67
  1934.9 35.3 %reduce-scatter.11.cloned.1.call-done = f32[1024,512]{1,0:T(8,128)} async-done(((f32[1024,2048]{1,0:T(8,128)}), f32[1024,512]{1,0:T(8,128)}) %reduce-scatter.11.cloned.1.call-update) | async-done | bytes 2097168 | tf_op jit(solution)/shard_map/reduce_scatter | solution.py:279
  1974.3 58.3 %all-reduce.77.cloned.1.call-done = (f32[4,176,176]{2,1,0:T(8,128)}, f32[4,176,176]{2,1,0:T(8,128)}) async-done(((f32[4,176,176]{2,1,0:T(8,128)}, f32[4,176,176]{2,1,0:T(8,128)}), (f32[4,176,176]{2,1,0:T(8,128)}, f32[4,176,176]{2,1,0:T(8,128)})) %all-reduce.77.cloned.1.call-update) | async-done | bytes 991248 | tf_op jit(solution)/shard_map/psum | solution.py:304
  2032.5 63.4 %reduce-scatter.17.cloned.1.call-done = f32[704,256]{1,0:T(8,128)} async-done(((f32[704,2048]{1,0:T(8,128)}), f32[704,256]{1,0:T(8,128)}) %reduce-scatter.17.cloned.1.call-update) | async-done | bytes 720912 | tf_op jit(solution)/shard_map/reduce_scatter | solution.py:289
  2096.0 63.0 %reduce-scatter.13.cloned.1.call-done = f32[256,704]{0,1:T(8,128)} async-done(((f32[2048,704]{0,1:T(8,128)}), f32[256,704]{0,1:T(8,128)}) %reduce-scatter.13.cloned.1.call-update) | async-done | bytes 720912 | tf_op jit(solution)/shard_map/reduce_scatter | solution.py:287
  2158.9 63.3 %reduce-scatter.15.cloned.1.call-done = f32[256,704]{0,1:T(8,128)} async-done(((f32[2048,704]{0,1:T(8,128)}), f32[256,704]{0,1:T(8,128)}) %reduce-scatter.15.cloned.1.call-update) | async-done | bytes 720912 | tf_op jit(solution)/shard_map/reduce_scatter | solution.py:288
  2222.2 96.3 %reduce-scatter.19.cloned.1.call-done = f32[256,1536]{1,0:T(8,128)} async-done(((f32[2048,1536]{1,0:T(8,128)}), f32[256,1536]{1,0:T(8,128)}) %reduce-scatter.19.cloned.1.call-update) | async-done | bytes 1572880 | tf_op jit(solution)/shard_map/reduce_scatter | solution.py:290
  2318.5 96.3 %reduce-scatter.21.cloned.1.call-done = f32[256,1536]{1,0:T(8,128)} async-done(((f32[2048,1536]{1,0:T(8,128)}), f32[256,1536]{1,0:T(8,128)}) %reduce-scatter.21.cloned.1.call-update) | async-done | bytes 1572880 | tf_op jit(solution)/shard_map/reduce_scatter | solution.py:291
  2414.8 96.4 %reduce-scatter.23.cloned.1.call-done = f32[1536,256]{1,0:T(8,128)} async-done(((f32[1536,2048]{1,0:T(8,128)}), f32[1536,256]{1,0:T(8,128)}) %reduce-scatter.23.cloned.1.call-update) | async-done | bytes 1572880 | tf_op jit(solution)/shard_map/reduce_scatter | solution.py:292
  (631 shorter events, 1002.5 us)
Async XLA Ops:
  7.2 139.5 %copy-start = (bf16[4,176,176]{2,1,0:T(8,128)(2,1)S(1)}, bf16[4,176,176]{2,1,0:T(8,128)(2,1)}, u32[]{:S(2)}) copy-start(bf16[4,176,176]{2,1,0:T(8,128)(2,1)} %param.35) | copy-start | bytes 743428
  7.2 81.9 %all-gather.14.cloned.1.call-start = ((), (), s32[]{:S(2)}) async-start(), calls=%async_computation.8 | async-start | bytes 5242880 | tf_op jit(solution)/shard_map/all_gather | solution.py:95
  7.9 115.7 %all-gather.16.cloned.1.call-start = ((), (), s32[]{:S(2)}) async-start(), calls=%async_computation.9 | async-start | bytes 3244032 | tf_op jit(solution)/shard_map/all_gather | solution.py:101
  8.7 516.8 %all-gather.18.cloned.1.call-start = ((), (), s32[]{:S(2)}) async-start(), calls=%async_computation.10 | async-start | bytes 3244032 | tf_op jit(solution)/shard_map/all_gather | solution.py:100
  9.4 525.8 %all-gather.20.cloned.1.call-start = ((), (), s32[]{:S(2)}) async-start(), calls=%async_computation.11 | async-start | bytes 3244032 | tf_op jit(solution)/shard_map/all_gather | solution.py:102
  10.0 824.0 %all-reduce.73.cloned.1.call-start = ((), (), s32[]{:S(2)}) async-start(), calls=%async_computation.12 | async-start | bytes 16777216 | tf_op jit(solution)/shard_map/psum | solution.py:181
  22.8 73.2 %copy-start.51 = (f32[4,1,512]{2,1,0:T(1,128)}, f32[4,1,512]{2,1,0:T(1,128)S(1)}, u32[]{:S(2)}) copy-start(f32[4,1,512]{2,1,0:T(1,128)S(1)} %convert_element_type.180) | copy-start | bytes 24580
  23.8 113.2 %copy-start.71 = (f32[704]{0:T(1024)}, f32[704]{0:T(1024)S(1)}, u32[]{:S(2)}) copy-start(f32[704]{0:T(1024)S(1)} %get-tuple-element.255) | copy-start | bytes 8452
  23.8 113.2 %copy-start.73 = (f32[704]{0:T(1024)}, f32[704]{0:T(1024)S(1)}, u32[]{:S(2)}) copy-start(f32[704]{0:T(1024)S(1)} %get-tuple-element.256) | copy-start | bytes 8452
  23.8 113.2 %copy-start.75 = (f32[704]{0:T(1024)}, f32[704]{0:T(1024)S(1)}, u32[]{:S(2)}) copy-start(f32[704]{0:T(1024)S(1)} %get-tuple-element.257) | copy-start | bytes 8452
  23.8 113.2 %copy-start.77 = (f32[704]{0:T(1024)}, f32[704]{0:T(1024)S(1)}, u32[]{:S(2)}) copy-start(f32[704]{0:T(1024)S(1)} %get-tuple-element.258) | copy-start | bytes 8452
  24.5 993.4 %copy-start.49 = (f32[704]{0:T(1024)}, f32[704]{0:T(1024)S(1)}, u32[]{:S(2)}) copy-start(f32[704]{0:T(1024)S(1)} %fusion.94) | copy-start | bytes 8452
  132.6 4.3 collective-permute-start
  135.6 35.3 %copy-start.47 = (f32[4,256]{1,0:T(4,128)}, f32[4,256]{1,0:T(4,128)S(1)}, u32[]{:S(2)}) copy-start(f32[4,256]{1,0:T(4,128)S(1)} %get-tuple-element.377) | copy-start | bytes 12292
  300.1 37.3 %copy-start.67 = (f32[4,1,704]{2,1,0:T(1,128)S(1)}, f32[4,1,704]{2,1,0:T(1,128)}, u32[]{:S(2)}) copy-start(f32[4,1,704]{2,1,0:T(1,128)} %slice.752) | copy-start | bytes 33796
  544.3 338.0 %all-gather.22.cloned.1.call-start = ((), (), s32[]{:S(2)}) async-start(), calls=%async_computation.13 | async-start | bytes 7077888 | tf_op jit(solution)/shard_map/all_gather | solution.py:103
  544.9 384.8 %all-gather.24.cloned.1.call-start = ((), (), s32[]{:S(2)}) async-start(), calls=%async_computation.14 | async-start | bytes 7077888 | tf_op jit(solution)/shard_map/all_gather | solution.py:104
  545.6 432.7 %all-gather.26.cloned.1.call-start = ((), (), s32[]{:S(2)}) async-start(), calls=%async_computation.15 | async-start | bytes 7077888 | tf_op jit(solution)/shard_map/all_gather | solution.py:105
  546.4 760.5 %all-reduce.75.cloned.1.call-start = ((), (), s32[]{:S(2)}) async-start(), calls=%async_computation.17 | async-start | bytes 16777216 | tf_op jit(solution)/shard_map/psum | solution.py:200
  558.5 748.4 %copy-start.42 = (f32[4,1,512]{2,1,0:T(1,128)}, f32[4,1,512]{2,1,0:T(1,128)S(1)}, u32[]{:S(2)}) copy-start(f32[4,1,512]{2,1,0:T(1,128)S(1)} %convert_element_type.181) | copy-start | bytes 24580
  839.9 467.0 %copy-start.53 = (f32[1024]{0:T(1024)}, f32[1024]{0:T(1024)S(1)}, u32[]{:S(2)}) copy-start(f32[1024]{0:T(1024)S(1)} %fusion.101) | copy-start | bytes 12292
  1017.8 913.5 %reduce-scatter.9.cloned.1.call-start = ((), (), s32[]{:S(2)}) async-start(), calls=%async_computation.16 | async-start | bytes 10485760 | tf_op jit(solution)/shard_map/reduce_scatter | solution.py:189
  1101.7 868.6 %reduce-scatter.11.cloned.1.call-start = ((), (), s32[]{:S(2)}) async-start(), calls=%async_computation.18 | async-start | bytes 10485760 | tf_op jit(solution)/shard_map/reduce_scatter | solution.py:279
  1519.2 30.4 %copy-start.66 = (f32[4,1,704]{2,1,0:T(1,128)S(1)}, f32[4,1,704]{2,1,0:T(1,128)}, u32[]{:S(2)}) copy-start(f32[4,1,704]{2,1,0:T(1,128)} %slice.804) | copy-start | bytes 33796
  1806.3 5.0 collective-permute-start.1
  1822.9 209.6 %all-reduce.77.cloned.1.call-start = ((), (), s32[]{:S(2)}) async-start(), calls=%async_computation.25 | async-start | bytes 2883584 | tf_op jit(solution)/shard_map/psum | solution.py:304
  1827.7 268.3 %reduce-scatter.17.cloned.1.call-start = ((), (), s32[]{:S(2)}) async-start(), calls=%async_computation.21 | async-start | bytes 6488064 | tf_op jit(solution)/shard_map/reduce_scatter | solution.py:289
  1836.0 322.9 %reduce-scatter.13.cloned.1.call-start = ((), (), s32[]{:S(2)}) async-start(), calls=%async_computation.19 | async-start | bytes 6488064 | tf_op jit(solution)/shard_map/reduce_scatter | solution.py:287
  1844.7 377.6 %reduce-scatter.15.cloned.1.call-start = ((), (), s32[]{:S(2)}) async-start(), calls=%async_computation.20 | async-start | bytes 6488064 | tf_op jit(solution)/shard_map/reduce_scatter | solution.py:288
  1854.2 464.3 %reduce-scatter.19.cloned.1.call-start = ((), (), s32[]{:S(2)}) async-start(), calls=%async_computation.22 | async-start | bytes 14155776 | tf_op jit(solution)/shard_map/reduce_scatter | solution.py:290
  1866.7 548.1 %reduce-scatter.21.cloned.1.call-start = ((), (), s32[]{:S(2)}) async-start(), calls=%async_computation.23 | async-start | bytes 14155776 | tf_op jit(solution)/shard_map/reduce_scatter | solution.py:291
  1879.5 631.7 %reduce-scatter.23.cloned.1.call-start = ((), (), s32[]{:S(2)}) async-start(), calls=%async_computation.24 | async-start | bytes 14155776 | tf_op jit(solution)/shard_map/reduce_scatter | solution.py:292
  (101 other events, 679.6 us)
Sparse Core Ops, SparseCore 0:
  9.6 79.4 all-gather.13
  91.0 32.6 all-gather.15
  125.5 31.8 all-gather.17
  159.2 31.6 all-gather.19
  544.4 289.5 all-reduce.72
  835.8 46.4 all-gather.21
  884.2 45.5 all-gather.23
  931.6 46.6 all-gather.25
  1018.0 288.8 all-reduce.74
  1309.1 145.0 reduce-scatter.8
  1823.0 147.1 reduce-scatter.10
  1973.9 58.5 all-reduce.76
  2036.9 58.9 reduce-scatter.16
  2099.8 59.0 reduce-scatter.12
  2163.2 58.9 reduce-scatter.14
  2226.2 92.2 reduce-scatter.18
  2322.4 92.3 reduce-scatter.20
  2418.8 92.3 reduce-scatter.22
where the time goes:
time: 2550 us; the launch traced here: 2520 us
  waiting for transfers between devices  1260 us (49%)
  local copies, waits for them, and re-layouts  705 us (28%)
  other arithmetic  262 us (10%)
  matrix products  193 us (8%)
  blocking collectives  82.7 us (3%)
    psum x1, waiting for transfers between devices, shards(): rec_total = lax.psum(rec_part, 'tp')  275 us
    slice x57, local copies, waits for them, and re-layouts, shards(): lax.associative_scan(combine, (next_coef, state_direct), reverse=True, ax...  215 us
    psum x1, waiting for transfers between devices, shards(): mid_norm_grad = lax.psum(mid_part, 'tp')  205 us
    slice x52, local copies, waits for them, and re-layouts, shards(): lax.associative_scan(combine, (coeffs, inputs), axis=1)  128 us
    pad x28, local copies, waits for them, and re-layouts, shards(): lax.associative_scan(combine, (coeffs, inputs), axis=1)  110 us
    pad x28, local copies, waits for them, and re-layouts, shards(): lax.associative_scan(combine, (next_coef, state_direct), reverse=True, ax...  108 us
    reduce_scatter x1, waiting for transfers between devices, shards(): lax.psum_scatter(grad_down, ('fsdp', 'ctx'), scatter_dimension=1, tiled=T...  96.4 us
    reduce_scatter x1, waiting for transfers between devices, shards(): lax.psum_scatter(grad_up, ('fsdp', 'ctx'), scatter_dimension=0, tiled=True)  96.3 us
  transfers between devices with their start and end apart: 20, of which 15 were waited for; matrix products, arithmetic and copies ran while one was open for 43% of the time, Pallas kernels for 0%

commit v1 on v0

v1 whole, which is shorter than its diff:
```python
import functools

import jax
import jax.numpy as jnp
from jax import lax
from jax.experimental import pallas as pl
from jax.experimental.pallas import tpu as pltpu
from jax.sharding import PartitionSpec as P

CONV = 4
EPS = 1e-06
LANES = 128
SEGS = 8
F32 = jnp.float32
BF16 = jnp.bfloat16


def xor_permute(value, axis, bit):
    count = lax.axis_size(axis)
    return lax.ppermute(value, axis, [(i, i ^ bit) for i in range(count)])


def quad_mesh():
    return lax.axis_size("fsdp") == 2 and lax.axis_size("ctx") == 4


def own_place():
    place = lax.axis_index("ctx")
    return lax.axis_index("fsdp"), place // 2, place % 2


def gather_rows(shard):
    rows, width = shard.shape
    if not quad_mesh():
        return lax.all_gather(shard, ("fsdp", "ctx"), axis=0, tiled=True)
    half = rows // 2
    own_x, own_y, own_c = own_place()
    from_x = xor_permute(shard, "fsdp", 1)
    from_y = xor_permute(shard, "ctx", 2)
    corner_top = xor_permute(from_y[:half], "fsdp", 1)
    corner_low = xor_permute(from_x[half:], "ctx", 2)
    quad = jnp.zeros((2, 2, rows, width), shard.dtype)

    def place(buffer, block, at_x, at_y, row):
        return lax.dynamic_update_slice(buffer, block[None, None], (at_x, at_y, row, 0))

    quad = place(quad, shard, own_x, own_y, 0)
    quad = place(quad, from_x, 1 - own_x, own_y, 0)
    quad = place(quad, from_y, own_x, 1 - own_y, 0)
    quad = place(quad, corner_top, 1 - own_x, 1 - own_y, 0)
    quad = place(quad, corner_low, 1 - own_x, 1 - own_y, half)
    quad = quad.reshape(4, 1, rows, width)
    other = xor_permute(quad, "ctx", 1)
    full = jnp.zeros((4, 2, rows, width), shard.dtype)
    full = lax.dynamic_update_slice(full, quad, (0, own_c, 0, 0))
    full = lax.dynamic_update_slice(full, other, (0, 1 - own_c, 0, 0))
    return full.reshape(8 * rows, width)


def pick(value, index, axis):
    return lax.dynamic_index_in_dim(value, index, axis, keepdims=False)


def add_low(left, right):
    return (left.astype(F32) + right.astype(F32)).astype(BF16)


def scatter_rows(partial):
    if not quad_mesh():
        return lax.psum_scatter(
            partial, ("fsdp", "ctx"), scatter_dimension=0, tiled=True
        ).astype(F32)
    total, width = partial.shape
    rows = total // 8
    half = rows // 2
    own_x, own_y, own_c = own_place()
    cube = partial.reshape(4, 2, rows, width)
    got = xor_permute(pick(cube, 1 - own_c, 1), "ctx", 1)
    quad = add_low(pick(cube, own_c, 1), got).reshape(2, 2, rows, width)
    top, low = quad[:, :, :half], quad[:, :, half:]
    top_got = xor_permute(pick(top, 1 - own_x, 0), "fsdp", 1)
    low_got = xor_permute(pick(low, 1 - own_y, 1), "ctx", 2)
    top = add_low(pick(top, own_x, 0), top_got)
    low = add_low(pick(low, own_y, 1), low_got)
    top_last = xor_permute(pick(top, 1 - own_y, 0), "ctx", 2)
    low_last = xor_permute(pick(low, 1 - own_x, 0), "fsdp", 1)
    top = pick(top, own_y, 0).astype(F32) + top_last.astype(F32)
    low = pick(low, own_x, 0).astype(F32) + low_last.astype(F32)
    return jnp.concatenate([top, low], axis=0)


def total_over_tokens(value):
    if not quad_mesh():
        return lax.psum(value, ("fsdp", "ctx"))
    value = value + xor_permute(value, "ctx", 1)
    value = value + xor_permute(value, "fsdp", 1)
    return value + xor_permute(value, "ctx", 2)


def from_behind(value, axis, steps):
    count = lax.axis_size(axis)
    leading, last = (max(0, -steps), min(count, count - steps))
    return lax.ppermute(value, axis, [(source, source + steps) for source in range(leading, last)])


def entering(coef, state, backward):
    count, mine = lax.axis_size("ctx"), lax.axis_index("ctx")
    both = lax.all_gather(jnp.stack([coef, state]), "ctx")
    total = jnp.zeros_like(state)
    for step in range(count - 1):
        position = count - 1 - step if backward else step
        before = position > mine if backward else position < mine
        total = jnp.where(before, both[position, 0] * total + both[position, 1], total)
    return total


def dot_nt(left, right):
    return lax.dot_general(left, right, (((1,), (1,)), ((), ())), preferred_element_type=F32)


def dot_tn(left, right):
    return lax.dot_general(left, right, (((0,), (0,)), ((), ())), preferred_element_type=F32)


def dot_nn(left, right):
    return jnp.dot(left, right, preferred_element_type=F32)


GELU_C = 0.7978845608028654
GELU_A = 0.044715


def gelu_parts(values):
    square = values * values
    tanh = jnp.tanh(GELU_C * values * (1.0 + GELU_A * square))
    act = 0.5 * values * (1.0 + tanh)
    slope = 0.5 * (1.0 + tanh) + 0.5 * values * (1.0 - tanh * tanh) * GELU_C * (
        1.0 + 3.0 * GELU_A * square
    )
    return act, slope


def minus_expm1(value):
    series = 1.0 / 40320.0
    for factor in (5040.0, 720.0, 120.0, 24.0, 6.0, 2.0, 1.0):
        series = series * value + 1.0 / factor
    return jnp.where(value > -0.5, -value * series, 1.0 - jnp.exp(value))


def softplus(value):
    return jnp.maximum(value, 0.0) + jnp.log1p(jnp.exp(-jnp.abs(value)))


def sigmoid(value):
    return 1.0 / (1.0 + jnp.exp(-value))


def chunked(total, size, body):
    def step(index, carry):
        body(pl.multiple_of(index * size, size))
        return carry

    lax.fori_loop(0, total // size, step, 0)


def scan_rows(coef_tiles, value_tiles, coef_ref, value_ref, backward):
    tiles, rows, lanes = value_tiles.shape
    part = rows // SEGS

    def step(index, carry):
        at = part - 1 - index if backward else index
        rows_at = pl.ds(at, SEGS, stride=part)
        out = []
        for tile, (coef_run, value_run) in enumerate(carry):
            coef = coef_tiles[tile, rows_at, :]
            value_run = coef * value_run + value_tiles[tile, rows_at, :]
            coef_run = coef * coef_run
            coef_tiles[tile, rows_at, :] = coef_run
            value_tiles[tile, rows_at, :] = value_run
            out.append((coef_run, value_run))
        return tuple(out)

    start = (jnp.ones((SEGS, lanes), F32), jnp.zeros((SEGS, lanes), F32))
    ends = lax.fori_loop(0, part, step, (start,) * tiles)
    order = list(range(SEGS))[::-1] if backward else list(range(SEGS))
    for tile, (coef_end, value_end) in enumerate(ends):
        columns = slice(tile * lanes, (tile + 1) * lanes)
        coef_in, value_in = jnp.ones((1, lanes), F32), jnp.zeros((1, lanes), F32)
        for seg in order:
            window = pl.ds(seg * part, part)
            coef = coef_tiles[tile, window, :]
            value_ref[window, columns] = value_tiles[tile, window, :] + coef * value_in
            coef_ref[window, columns] = coef * coef_in
            value_in = coef_end[seg : seg + 1] * value_in + value_end[seg : seg + 1]
            coef_in = coef_end[seg : seg + 1] * coef_in


def shifted(ref, at, count, offset):
    if offset % 8 == 0:
        return ref[pl.ds(at + offset, count), :]
    return ref[pl.ds(at, count + 8), :][offset : offset + count]


def put_tiles(tiles_ref, window, value):
    for tile in range(tiles_ref.shape[0]):
        tiles_ref[tile, window, :] = value[:, tile * LANES : (tile + 1) * LANES]


def forward_kernel(
    x_ref, edge_ref, mask_ref, vec_ref, gate_ref,
    conv_ref, rate_ref, input_ref, coef_ref, state_ref,
    ext, pre, coef_tiles, value_tiles,
):
    rows, width = x_ref.shape
    ext[0:8, :] = edge_ref[...].astype(F32)
    ext[8:, :] = x_ref[...].astype(F32)
    chunk = 32

    def conv(at):
        total = vec_ref[4:5, :]
        for tap in range(CONV):
            total = total + vec_ref[tap : tap + 1, :] * shifted(ext, at, chunk, 8 - tap) * mask_ref[
                pl.ds(at, chunk), tap : tap + 1
            ]
        conv_ref[pl.ds(at, chunk), :] = total.astype(BF16)

    chunked(rows, chunk, conv)
    pre[...] = dot_nn(conv_ref[...], gate_ref[...])
    decay = -8.0 * softplus(vec_ref[7:8, :])

    def gates(at):
        window = pl.ds(at, chunk)
        rate = sigmoid(pre[window, :width] + vec_ref[5:6, :])
        gate = sigmoid(pre[window, width:] + vec_ref[6:7, :])
        log_a = decay * rate
        rate_ref[window, :] = rate
        input_ref[window, :] = gate
        put_tiles(coef_tiles, window, jnp.exp(log_a) * mask_ref[window, 1:2])
        put_tiles(
            value_tiles, window, jnp.sqrt(minus_expm1(2.0 * log_a)) * gate * conv_ref[window, :].astype(F32)
        )

    chunked(rows, chunk, gates)
    scan_rows(coef_tiles, value_tiles, coef_ref, state_ref, False)


def forward_call(x_branch, edge, masks, vectors, gates):
    count, rows, width = x_branch.shape
    seq = lambda *tail: pl.BlockSpec((None, *tail), lambda i: (i, 0, 0))
    whole = lambda *shape: pl.BlockSpec(shape, lambda i: (0, 0))
    wide = jax.ShapeDtypeStruct((count, rows, width), F32)
    return pl.pallas_call(
        forward_kernel,
        grid=(count,),
        in_specs=[
            seq(rows, width), seq(8, width), seq(rows, LANES), whole(8, width), whole(width, 2 * width)
        ],
        out_specs=[seq(rows, width)] * 5,
        out_shape=[jax.ShapeDtypeStruct((count, rows, width), BF16), wide, wide, wide, wide],
        scratch_shapes=[
            pltpu.VMEM((rows + 8, width), F32),
            pltpu.VMEM((rows, 2 * width), F32),
            pltpu.VMEM((width // LANES, rows, LANES), F32),
            pltpu.VMEM((width // LANES, rows, LANES), F32),
        ],
        cost_estimate=pl.CostEstimate(
            flops=4 * count * rows * width * width,
            bytes_accessed=count * rows * width * 20,
            transcendentals=count * rows * width * 6,
        ),
        name="conv_gates_scan",
    )(x_branch, edge, masks, vectors, gates)


def reverse_kernel(
    grad_ref, y_ref, state_ref, rate_ref, mask_ref, vec_ref, y_grad_ref, direct_ref, coef_ref, value_ref,
    coef_tiles, value_tiles,
):
    rows, width = grad_ref.shape
    decay = -8.0 * softplus(vec_ref[7:8, :])

    def body(at):
        window = pl.ds(at, 32)
        act, slope = gelu_parts(y_ref[window, :])
        grad = grad_ref[window, :]
        y_grad_ref[window, :] = (grad * state_ref[window, :] * slope).astype(BF16)
        direct = grad * act
        coef = jnp.exp(decay * rate_ref[window, :]) * mask_ref[window, 1:2]
        direct_ref[window, :] = direct
        put_tiles(coef_tiles, window, coef)
        put_tiles(value_tiles, window, coef * direct)

    chunked(rows, 32, body)
    scan_rows(coef_tiles, value_tiles, coef_ref, value_ref, True)


def reverse_call(grad, y_pre, states, rate, masks, vectors):
    count, rows, width = grad.shape
    seq = lambda *tail: pl.BlockSpec((None, *tail), lambda i: (i, 0, 0))
    whole = lambda *shape: pl.BlockSpec(shape, lambda i: (0, 0))
    wide = jax.ShapeDtypeStruct((count, rows, width), F32)
    return pl.pallas_call(
        reverse_kernel,
        grid=(count,),
        in_specs=[seq(rows, width)] * 4 + [seq(rows, LANES), whole(8, width)],
        out_specs=[seq(rows, width)] * 4,
        out_shape=[jax.ShapeDtypeStruct((count, rows, width), BF16), wide, wide, wide],
        scratch_shapes=[pltpu.VMEM((width // LANES, rows, LANES), F32)] * 2,
        cost_estimate=pl.CostEstimate(
            flops=40 * count * rows * width,
            bytes_accessed=count * rows * width * 30,
            transcendentals=count * rows * width * 2,
        ),
        name="reverse_scan",
    )(grad, y_pre, states, rate, masks, vectors)


def backward_kernel(
    direct_ref, coef_ref, value_ref, enter_ref, state_ref, before_ref, rate_ref, input_ref, conv_ref,
    x_ref, edge_ref, mask_ref, ahead_ref, vec_ref, gate_ref,
    branch_ref, tail_ref, head_ref, sums_ref, gate_grad_ref,
    ext, states, value, both, conv_grad,
):
    rows, width = direct_ref.shape
    chunk = 32
    decay = -8.0 * softplus(vec_ref[7:8, :])
    lean = -8.0 * sigmoid(vec_ref[7:8, :])
    first = pl.program_id(0) == 0

    ext[0:8, :] = edge_ref[...].astype(F32)
    ext[8:, :] = x_ref[...].astype(F32)
    states[7:8, :] = before_ref[0:1, :]
    states[8:, :] = state_ref[...]
    value[0:rows, :] = value_ref[...] + coef_ref[...] * enter_ref[0:1, :]
    value[rows : rows + 1, :] = enter_ref[0:1, :]

    @pl.when(first)
    def _():
        sums_ref[...] = jnp.zeros_like(sums_ref)

    zero = jnp.zeros((8, width), F32)

    def fold(array):
        return array.reshape(chunk // 8, 8, width).sum(axis=0)

    def body(index, carry):
        rate_sum, input_sum, decay_sum = carry
        at = pl.multiple_of(index * chunk, chunk)
        window = pl.ds(at, chunk)
        grad = direct_ref[window, :] + shifted(value, at, chunk, 1)
        rate, gate = rate_ref[window, :], input_ref[window, :]
        conv = conv_ref[window, :].astype(F32)
        log_a = decay * rate
        decays = jnp.exp(log_a)
        root = jnp.sqrt(minus_expm1(2.0 * log_a))
        scale_grad = grad * conv
        log_grad = grad * shifted(states, at, chunk, 7) * mask_ref[window, 1:2] * decays
        log_grad = log_grad - scale_grad * gate * (decays * decays) / root
        rate_grad = (log_grad * decay * rate * (1.0 - rate)).astype(BF16)
        input_grad = (scale_grad * root * gate * (1.0 - gate)).astype(BF16)
        both[window, :width] = rate_grad
        both[window, width:] = input_grad
        conv_grad[window, :] = grad * root * gate
        return (
            rate_sum + fold(rate_grad.astype(F32)),
            input_sum + fold(input_grad.astype(F32)),
            decay_sum + fold(log_grad * rate),
        )

    rate_sum, input_sum, decay_sum = lax.fori_loop(0, rows // chunk, body, (zero, zero, zero))
    sums_ref[0:8, :] += rate_sum
    sums_ref[8:16, :] += input_sum
    sums_ref[16:24, :] += decay_sum * lean

    gate_part = dot_tn(conv_ref[...], both[...])

    @pl.when(first)
    def _():
        gate_grad_ref[...] = gate_part

    @pl.when(jnp.logical_not(first))
    def _():
        gate_grad_ref[...] += gate_part

    rounded = (conv_grad[0:rows, :] + dot_nt(both[...], gate_ref[...])).astype(BF16).astype(F32)
    conv_grad[0:rows, :] = rounded
    conv_grad[rows:, :] = jnp.zeros_like(conv_grad[rows:, :])
    head_ref[...] = rounded[0:8, :]

    def branch(at):
        window = pl.ds(at, chunk)
        total = jnp.zeros((chunk, width), F32)
        grad = conv_grad[window, :]
        sums_ref[24:32, :] += fold(grad)
        for tap in range(CONV):
            total = total + vec_ref[tap : tap + 1, :] * shifted(conv_grad, at, chunk, tap) * ahead_ref[
                window, tap : tap + 1
            ]
            behind = shifted(ext, at, chunk, 8 - tap) * mask_ref[window, tap : tap + 1]
            sums_ref[32 + 8 * tap : 40 + 8 * tap, :] += fold(grad * behind)
        branch_ref[window, :] = total.astype(BF16)
        tail_ref[...] = total[chunk - 8 :, :]

    chunked(rows, chunk, branch)


def backward_call(
    direct, coef, value, enter, states, before, rate, gate, conv, x_branch, edge, masks, ahead, vectors, gates
):
    count, rows, width = direct.shape
    seq = lambda *tail: pl.BlockSpec((None, *tail), lambda i: (i, 0, 0))
    whole = lambda *shape: pl.BlockSpec(shape, lambda i: (0, 0))
    return pl.pallas_call(
        backward_kernel,
        grid=(count,),
        in_specs=[
            seq(rows, width), seq(rows, width), seq(rows, width), seq(8, width),
            seq(rows, width), seq(8, width), seq(rows, width), seq(rows, width), seq(rows, width),
            seq(rows, width), seq(8, width), seq(rows, LANES), seq(rows, LANES),
            whole(8, width), whole(width, 2 * width),
        ],
        out_specs=[
            seq(rows, width), seq(8, width), seq(8, width), whole(64, width), whole(width, 2 * width)
        ],
        out_shape=[
            jax.ShapeDtypeStruct((count, rows, width), BF16),
            jax.ShapeDtypeStruct((count, 8, width), F32),
            jax.ShapeDtypeStruct((count, 8, width), F32),
            jax.ShapeDtypeStruct((64, width), F32),
            jax.ShapeDtypeStruct((width, 2 * width), F32),
        ],
        scratch_shapes=[
            pltpu.VMEM((rows + 8, width), F32),
            pltpu.VMEM((rows + 8, width), F32),
            pltpu.VMEM((rows + 8, width), F32),
            pltpu.VMEM((rows, 2 * width), BF16),
            pltpu.VMEM((rows + 8, width), F32),
        ],
        cost_estimate=pl.CostEstimate(
            flops=8 * count * rows * width * width,
            bytes_accessed=count * rows * width * 34,
            transcendentals=count * rows * width * 4,
        ),
        name="gates_backward",
    )(direct, coef, value, enter, states, before, rate, gate, conv, x_branch, edge, masks, ahead, vectors, gates)


def block_diagonal(rate_gate, input_gate, padded):
    heads, size, _ = rate_gate.shape

    def spread(gate):
        rows = [
            jnp.pad(gate[head], ((0, 0), (head * size, padded - (head + 1) * size)))
            for head in range(heads)
        ]
        rows.append(jnp.zeros((padded - heads * size, padded), gate.dtype))
        return jnp.concatenate(rows, axis=0)

    return jnp.concatenate([spread(rate_gate), spread(input_gate)], axis=1)


def shards(
    block_in, seg_ids, out_cot, norm_gain, mid_gain, gelu_proj, scan_proj, out_proj, gate_proj,
    up_proj, down_proj, conv_kernel, conv_bias, rate_gate, input_gate, rate_bias, input_bias,
    decay_param,
):
    seq_count, tok_count, part_width = block_in.shape
    row_count = seq_count * tok_count
    rec_width = gelu_proj.shape[1]
    hidden_width = gate_proj.shape[1]
    heads, size, _ = rate_gate.shape
    padded = -(-rec_width // LANES) * LANES
    extra = padded - rec_width

    def widen(value):
        return jnp.pad(value, ((0, 0), (0, extra)))

    def split(value):
        return value.reshape(seq_count, tok_count, value.shape[-1])

    x_full = lax.all_gather(block_in.reshape(row_count, part_width), "tp", axis=1, tiled=True)
    gains = lax.all_gather(jnp.stack([norm_gain, mid_gain]), "tp", axis=1, tiled=True).astype(F32)
    gain_one, gain_two = gains[0:1], gains[1:2]
    full_width = x_full.shape[1]

    w_in = gather_rows(jnp.concatenate([widen(gelu_proj), widen(scan_proj)], axis=1))
    w_out = gather_rows(widen(out_proj.T))
    w_ff = gather_rows(jnp.concatenate([gate_proj, up_proj], axis=1))
    w_down = gather_rows(down_proj.T)

    margin = CONV - 1
    start_tok = lax.axis_index("ctx") * tok_count
    padded_ids = jnp.concatenate(
        [
            jnp.full((seq_count, margin), -1, jnp.int32),
            seg_ids,
            jnp.full((seq_count, margin), -2, jnp.int32),
        ],
        axis=1,
    )
    ids = lax.dynamic_slice_in_dim(padded_ids, start_tok, tok_count + 2 * margin, 1)
    own_ids = ids[:, margin : margin + tok_count]
    back = [ids[:, margin - k : margin - k + tok_count] == own_ids for k in range(CONV)]
    ahead = [ids[:, margin + k : margin + k + tok_count] == own_ids for k in range(CONV)]
    fill = ((0, 0), (0, 0), (0, LANES - CONV))
    back = jnp.pad(jnp.stack(back, axis=-1).astype(F32), fill)
    ahead_f = jnp.stack(ahead, axis=-1).astype(F32)
    ahead = jnp.pad(ahead_f, fill)

    vectors = widen(
        jnp.concatenate(
            [conv_kernel, conv_bias[None], rate_bias[None], input_bias[None], decay_param[None]], axis=0
        )
    )
    gates = block_diagonal(rate_gate, input_gate, padded)

    x_rows = x_full.astype(F32)
    scale_one = lax.rsqrt(jnp.mean(x_rows * x_rows, axis=-1, keepdims=True) + EPS)
    normed = (x_rows * scale_one * gain_one).astype(BF16)
    y_pre = split(dot_nn(normed, w_in[:, :padded]))
    x_branch = split(dot_nn(normed, w_in[:, padded:]).astype(BF16))

    prev_edge = from_behind(x_branch[:, tok_count - margin :, :], "ctx", 1)
    edge = jnp.pad(prev_edge, ((0, 0), (8 - margin, 0), (0, 0)))
    conv, rate, gate, coef, local = forward_call(x_branch, edge, back, vectors, gates)
    state_in = entering(coef[:, -1], local[:, -1], False)
    states = local + coef * state_in[:, None, :]
    y_act, _ = gelu_parts(y_pre)
    mixed_in = (states * y_act).astype(BF16).reshape(row_count, padded)

    rec_part = dot_nt(mixed_in, w_out).astype(BF16)
    rec_own = lax.psum_scatter(rec_part, "tp", scatter_dimension=1, tiled=True)
    mid_own = block_in.reshape(row_count, part_width).astype(F32) + rec_own.astype(F32)
    mid = lax.all_gather(mid_own.astype(BF16), "tp", axis=1, tiled=True).astype(F32)
    scale_two = lax.rsqrt(jnp.mean(mid * mid, axis=-1, keepdims=True) + EPS)
    normed_mid = (mid * scale_two * gain_two).astype(BF16)

    cot = out_cot.reshape(row_count, full_width)
    hid_grad = dot_nn(cot, w_down)
    pre = dot_nn(normed_mid, w_ff)
    gate_pre, up_pre = pre[:, :hidden_width], pre[:, hidden_width:]
    gate_act, gate_slope = gelu_parts(gate_pre)
    hidden = (gate_act * up_pre).astype(BF16)
    both_grad = jnp.concatenate(
        [(hid_grad * up_pre * gate_slope).astype(BF16), (hid_grad * gate_act).astype(BF16)], axis=1
    )
    mid_part = dot_nt(both_grad, w_ff)
    weighted = mid_part * gain_two
    mean_two = jnp.mean(weighted * mid, axis=-1, keepdims=True)
    back_two = (scale_two * weighted - mid * (scale_two * scale_two * scale_two * mean_two)).astype(BF16)
    gain_two_part = jnp.sum(mid_part * mid * scale_two, axis=0)
    back_own = lax.psum_scatter(back_two, "tp", scatter_dimension=1, tiled=True)
    col_start = lax.axis_index("tp") * part_width
    cot_own = lax.dynamic_slice_in_dim(cot, col_start, part_width, 1).astype(F32)
    mid_grad_own = cot_own + back_own.astype(F32)
    rec_grad = lax.all_gather(mid_grad_own.astype(BF16), "tp", axis=1, tiled=True)

    mlp_part = dot_nt(hidden, w_down).astype(BF16)
    grad_down = scatter_rows(dot_tn(cot, hidden).astype(BF16))
    grad_ff = scatter_rows(dot_tn(normed_mid, both_grad).astype(BF16))
    mlp_own = lax.psum_scatter(mlp_part, "tp", scatter_dimension=1, tiled=True)
    block_out = split((mid_own + mlp_own.astype(F32)).astype(BF16))

    mixed_grad = split(dot_nn(rec_grad, w_out))
    grad_out = scatter_rows(dot_tn(rec_grad, mixed_in).astype(BF16))
    y_grad, direct, tail_coef, tail_value = reverse_call(mixed_grad, y_pre, states, rate, back, vectors)
    enter = entering(tail_coef[:, 0], tail_value[:, 0], True)
    rows_of = lambda value: jnp.broadcast_to(value[:, None, :], (seq_count, 8, padded))
    branch, tail, head, sums, gate_grad = backward_call(
        direct, tail_coef, tail_value, rows_of(enter), states, rows_of(state_in), rate, gate, conv,
        x_branch, edge, back, ahead, vectors, gates,
    )
    next_edge = from_behind(head[:, :margin].astype(BF16), "ctx", -1).astype(F32)
    lead = jnp.concatenate([next_edge, jnp.zeros((seq_count, 8, padded), F32)], axis=1)
    for tap in range(1, CONV):
        reach = jnp.pad(lead[:, :tap], ((0, 0), (8 - tap, 0), (0, 0)))
        tail = tail + vectors[tap] * reach * ahead_f[:, tok_count - 8 :, tap : tap + 1]
    branch = lax.dynamic_update_slice(branch, tail.astype(BF16), (0, tok_count - 8, 0))
    in_grad = jnp.concatenate(
        [y_grad.reshape(row_count, padded), branch.reshape(row_count, padded)], axis=1
    )
    in_part = dot_nt(in_grad, w_in)
    weighted = in_part * gain_one
    mean_one = jnp.mean(weighted * x_rows, axis=-1, keepdims=True)
    back_one = (scale_one * weighted - x_rows * (scale_one * scale_one * scale_one * mean_one)).astype(BF16)
    gain_one_part = jnp.sum(in_part * x_rows * scale_one, axis=0)
    in_own = lax.psum_scatter(back_one, "tp", scatter_dimension=1, tiled=True)
    grad_in = split(mid_grad_own + in_own.astype(F32))
    grad_in_w = scatter_rows(dot_tn(normed, in_grad).astype(BF16))

    gain_parts = lax.psum_scatter(
        jnp.stack([gain_one_part, gain_two_part]), "tp", scatter_dimension=1, tiled=True
    )
    sums = sums.reshape(8, 8, padded).sum(axis=1)
    gain_parts = jnp.pad(gain_parts, ((0, 0), (0, padded - part_width)))
    small = total_over_tokens(jnp.concatenate([sums, gain_parts], axis=0))

    def diagonal(value, column):
        return jnp.stack(
            [
                value[h * size : (h + 1) * size, column + h * size : column + (h + 1) * size]
                for h in range(heads)
            ]
        )

    pieces = jnp.concatenate([diagonal(gate_grad, 0), diagonal(gate_grad, padded)], axis=2)
    pieces = total_over_tokens(pieces)

    return (
        block_out,
        grad_in,
        small[8, :part_width],
        small[9, :part_width],
        grad_in_w[:, :rec_width],
        grad_in_w[:, padded : padded + rec_width],
        grad_out[:, :rec_width].T,
        grad_ff[:, :hidden_width],
        grad_ff[:, hidden_width:],
        grad_down.T,
        small[4:8, :rec_width],
        small[3, :rec_width],
        pieces[:, :, :size],
        pieces[:, :, size:],
        small[0, :rec_width],
        small[1, :rec_width],
        small[2, :rec_width],
    )


def solution(mesh):
    rows, columns = P(("fsdp", "ctx"), "tp"), P("tp", ("fsdp", "ctx"))
    stream, vector, gate = P("fsdp", "ctx", "tp"), P("tp"), P("tp", None, None)
    in_specs = (
        stream, P("fsdp", None), P("fsdp", "ctx", None), vector, vector, rows, rows, columns, rows, rows,
        columns, P(None, "tp"), vector, gate, gate, vector, vector, vector,
    )
    out_specs = (
        stream, stream, vector, vector, rows, rows, columns, rows, rows, columns, P(None, "tp"), vector,
        gate, gate, vector, vector, vector,
    )
    return jax.shard_map(shards, mesh=mesh, in_specs=in_specs, out_specs=out_specs, check_vma=False)
```

time: 2550 us -> 909 us (0.36)
  waiting for transfers between devices: 1260 us -> 281 us
  local copies, waits for them, and re-layouts: 705 us -> 213 us
  other arithmetic: 262 us -> 87.3 us
  Pallas kernels: 0 us -> 77.6 us
  blocking collectives: 82.7 us -> 23.3 us
  matrix products: 193 us -> 148 us
  starting transfers between devices: 4.73 us -> 47.4 us
    psum x3 -> x0, waiting for transfers between devices: 539 us -> none  [the longest x1 275 us: shards(): rec_total = lax.psum(rec_part, 'tp')]
    reduce_scatter x8 -> x4, waiting for transfers between devices: 514 us -> 17.3 us  [the longest x1 17.3 us: shards(): rec_own = lax.psum_scatter(rec_part, 'tp', scatter_dimension=1, tiled=True)]
    slice x114 -> x23, local copies, waits for them, and re-layouts: 345 us -> 15.2 us  [the longest x4 4.52 us: gather_rows(): corner_low = xor_permute(from_x[half:], 'ctx', 2)]
    pad x56 -> x4, local copies, waits for them, and re-layouts: 217 us -> 4.8 us  [the longest x2 2.2 us: widen(): return jnp.pad(value, ((0, 0), (0, extra)))]
    ppermute x0 -> x46, waiting for transfers between devices: none -> 195 us  [xor_permute(): return lax.ppermute(value, axis, [(i, i ^ bit) for i in range(count)])]
    all_gather x7 -> x3, waiting for transfers between devices: 200 us -> 42.1 us  [the longest x1 29.2 us: shards(): lax.all_gather(mid_grad_own.astype(BF16), 'tp', axis=1, tiled=True)]
    add x47 -> x15, other arithmetic: 108 us -> 14.9 us  [the longest x4 4.01 us: scatter_rows(): top = pick(top, own_y, 0).astype(F32) + top_last.astype(F32)]
    pallas_call x0 -> x3, Pallas kernels: none -> 77.6 us  [the longest x1 32.2 us: backward_call(): pl.pallas_call(backward_kernel, grid=(count,), in_specs=[seq(rows, width)...]
  transfers between devices with their start and end apart: 20 -> 56, of which waited for: 15 -> 27; matrix products, arithmetic and copies ran while one was open for 43% -> 38% of each run, Pallas kernels for 0% -> 6%
where the time goes in v1:
time: 909 us; the launch traced here: 894 us
  waiting for transfers between devices  281 us (31%)
  local copies, waits for them, and re-layouts  213 us (23%)
  matrix products  148 us (16%)
  other arithmetic  87.3 us (10%)
  Pallas kernels  77.6 us (9%)
  starting transfers between devices  47.4 us (5%)
  blocking collectives  23.3 us (3%)
  between operations  16.1 us (2%)
    ppermute x46, waiting for transfers between devices, xor_permute(): return lax.ppermute(value, axis, [(i, i ^ bit) for i in range(count)])  195 us
    unnamed x148, local copies, waits for them, and re-layouts  55.5 us
    dot_general x5, matrix products, dot_nn(): return jnp.dot(left, right, preferred_element_type=F32)  54.1 us
    dot_general x4, matrix products, dot_nt(): lax.dot_general(left, right, (((1,), (1,)), ((), ())), preferred_element_...  49.2 us
    dot_general x4, matrix products, dot_tn(): lax.dot_general(left, right, (((0,), (0,)), ((), ())), preferred_element_...  45.1 us
    ppermute x46, starting transfers between devices, xor_permute(): return lax.ppermute(value, axis, [(i, i ^ bit) for i in range(count)])  41.9 us
    pallas_call x1, Pallas kernels, backward_call(): pl.pallas_call(backward_kernel, grid=(count,), in_specs=[seq(rows, width)...  32.2 us
    all_gather x1, waiting for transfers between devices, shards(): lax.all_gather(mid_grad_own.astype(BF16), 'tp', axis=1, tiled=True)  29.2 us
  transfers between devices with their start and end apart: 56, of which 27 were waited for; matrix products, arithmetic and copies ran while one was open for 38% of the time, Pallas kernels for 6%

profile of v1, /device:TPU:10, one launch (start us, length us, event | category | flops | bytes accessed | tf_op | source)
XLA Modules:
  0.0 894.1 jit_solution(2259467869639818254)
XLA Ops:
  21.6 8.6 collective-permute-done
  67.2 12.3 %all_gather.25 = bf16[2,2048]{1,0:T(2,128)(2,1)S(1)} all-gather(bf16[2,512]{1,0:T(2,128)(2,1)} %pad_maximum_fusion.13), channel_id=1, replica_groups=mesh['fsdp'=2,'ctx'=4,'tp'=4] {'tp'}, dimensions={1}, use_global_device_ids=true | all-gather | bytes 10240 | tf_op jit(solution)/shard_map/all_gather | solution.py:482
  123.5 27.8 %conv_gates_scan.1 = (bf16[4,256,768]{2,1,0:T(8,128)(2,1)}, f32[4,256,768]{2,1,0:T(8,128)}, f32[4,256,768]{2,1,0:T(8,128)}, f32[4,256,768]{2,1,0:T(8,128)}, f32[4,256,768]{2,1,0:T(8,128)}) custom-call(bf16[4,256,768]{2,1,0:T(8,128)(2,1)} %bitcast.367, bf16[4,8,768]{2,1,0:T(8,128)(2,1)} %pad.73.edge_ref, f32[4,256,128]{2,1,0:T(8,128)} %pad_convert_fusion.mask_ref, ...), custom_call_target="tpu_custom_call" | custom-call | flops 2415919104 | bytes 15728640 | tf_op jit(solution)/shard_map/conv_gates_scan/pallas_call | solution.py:252
  180.3 28.7 %collective-permute-done.12 = bf16[256,3072]{1,0:T(8,128)(2,1)S(1)} collective-permute-done((bf16[256,3072]{1,0:T(8,128)(2,1)S(1)}, bf16[256,3072]{1,0:T(8,128)(2,1)S(1)}, u32[]{:S(2)}, u32[]{:S(2)}) %collective-permute-start.12) | collective-permute-done | bytes 1572896 | tf_op jit(solution)/shard_map/ppermute | solution.py:20
  214.7 13.5 %collective-permute-done.13 = bf16[128,3072]{1,0:T(8,128)(2,1)S(1)} collective-permute-done((bf16[128,3072]{1,0:T(8,128)(2,1)S(1)}, bf16[128,3072]{1,0:T(8,128)(2,1)S(1)}, u32[]{:S(2)}, u32[]{:S(2)}) %collective-permute-start.13) | collective-permute-done | bytes 786464 | tf_op jit(solution)/shard_map/ppermute | solution.py:20
  230.5 17.3 %reduce-scatter.8.cloned.1.call-done = bf16[1024,512]{1,0:T(8,128)(2,1)} async-done(((bf16[1024,2048]{1,0:T(8,128)(2,1)}), bf16[1024,512]{1,0:T(8,128)(2,1)}) %reduce-scatter.8.cloned.1.call-update) | async-done | bytes 1048592 | tf_op jit(solution)/shard_map/reduce_scatter | solution.py:532
  256.5 14.1 %collective-permute-done.16 = bf16[256,1536]{0,1:T(8,128)(2,1)} collective-permute-done((bf16[256,1536]{0,1:T(8,128)(2,1)}, bf16[256,1536]{0,1:T(8,128)(2,1)}, u32[]{:S(2)}, u32[]{:S(2)}) %collective-permute-start.16) | collective-permute-done | bytes 786464 | tf_op jit(solution)/shard_map/ppermute | solution.py:20
  316.4 12.9 %all-gather.8.cloned.1.call-done = bf16[1024,2048]{1,0:T(8,128)(2,1)} async-done(((bf16[1024,512]{1,0:T(8,128)(2,1)}), bf16[1024,2048]{1,0:T(8,128)(2,1)}) %all-gather.8.cloned.1.call-update) | async-done | bytes 4194320 | tf_op jit(solution)/shard_map/all_gather | solution.py:534
  332.8 18.4 %fusion.45 = f32[1024,3072]{1,0:T(8,128)} fusion(bf16[2048,3072]{1,0:T(8,128)(2,1)} %bitcast.338, bf16[1024,2048]{1,0:T(8,128)(2,1)S(1)} %copy-done.2, f32[2048]{0:T(1024)S(1)} %bitcast.386, f32[1024]{0:T(1024)S(1)} %add_rsqrt_fusion), kind=kOutput, calls=%fused_computation.101 | convolution fusion | flops 12893290496 | bytes 29372416 | tf_op jit(solution)/shard_map/dot_general | solution.py:126
  351.1 16.8 %fusion.21 = (bf16[1024,1536]{1,0:T(8,128)(2,1)}, bf16[1024,1536]{1,0:T(8,128)(2,1)}, bf16[1024,1536]{1,0:T(8,128)(2,1)S(1)}) fusion(f32[1024,3072]{1,0:T(8,128)} %fusion.45, bf16[1024,2048]{1,0:T(8,128)(2,1)S(1)} %bitcast.374, bf16[2048,1536]{1,0:T(8,128)(2,1)} %bitcast.56), kind=kOutput, calls=%fused_computation.40 | convolution fusion | flops 6480199680 | bytes 32505856 | tf_op jit(solution)/shard_map/dot_general | solution.py:126
  367.9 21.6 %fusion.16 = (f32[2048]{0:T(1024)S(1)}, f32[1024]{0:T(1024)S(1)}, f32[1024,2048]{1,0:T(8,128)}) fusion(bf16[1024,2048]{1,0:T(8,128)(2,1)} %all-gather.8.cloned.1.call-done, f32[1024]{0:T(1024)S(1)} %add_rsqrt_fusion, f32[2048]{0:T(1024)S(1)} %bitcast.387, bf16[2048,3072]{1,0:T(8,128)(2,1)} %bitcast.339, bf16[1024,1536]{1,0:T(8,128)(2,1)} %get-tuple-element.198, ...), kind=kOutput, calls=%fused_computation.28 | convolution fusion | flops 12912161792 | bytes 31481856 | tf_op jit(solution)/shard_map/dot_general | solution.py:118
  396.4 11.2 %fusion.17 = bf16[2048,1536]{0,1:T(8,128)(2,1)} fusion(bf16[1024,1536]{1,0:T(8,128)(2,1)S(1)} %get-tuple-element.199, bf16[1024,2048]{1,0:T(8,128)(2,1)} %bitcast.371), kind=kOutput, calls=%fused_computation.31 | convolution fusion | flops 6445596672 | bytes 13631488 | tf_op jit(solution)/shard_map/dot_general | solution.py:122
  407.6 11.1 %reshape.300 = bf16[4,2,256,1536]{2,1,0,3:T(2,128)(2,1)} reshape(bf16[2048,1536]{0,1:T(8,128)(2,1)} %fusion.17) | data formatting | bytes 12582912 | tf_op jit(solution)/shard_map/reshape | solution.py:77
  418.7 15.9 %constant_dynamic-slice_fusion.7 = (bf16[4,1,256,1536]{2,1,0,3:T(2,128)(2,1)}, bf16[4,1,256,1536]{2,1,0,3:T(2,128)(2,1)}) fusion(bf16[4,2,256,1536]{2,1,0,3:T(2,128)(2,1)} %reshape.300, s32[]{:T(128)S(6)} %select_n.224, s32[]{:T(128)S(6)} %select_n.225), kind=kLoop, calls=%fused_computation.185 | loop fusion | bytes 12582920 | tf_op jit(solution)/shard_map/jit(dynamic_index_in_dim)/dynamic_slice | solution.py:61
  434.6 15.4 %copy.368 = bf16[4,1,256,1536]{3,2,0,1:T(8,128)(2,1)} copy(bf16[4,1,256,1536]{2,1,0,3:T(2,128)(2,1)} %get-tuple-element.201) | data formatting | bytes 6291456
  450.0 11.0 %convolution_convert_fusion.3 = bf16[1024,2048]{1,0:T(8,128)(2,1)} fusion(bf16[1024,1536]{1,0:T(8,128)(2,1)S(1)} %get-tuple-element.199, bf16[2048,1536]{1,0:T(8,128)(2,1)} %bitcast.56), kind=kOutput, calls=%fused_computation.47 | convolution fusion | flops 6444548096 | bytes 13631488 | tf_op jit(solution)/shard_map/dot_general | solution.py:118
  462.9 19.6 %convolution_convert_fusion = bf16[2048,3072]{1,0:T(8,128)(2,1)} fusion(bf16[1024,1536]{1,0:T(8,128)(2,1)} %get-tuple-element.198, bf16[1024,1536]{1,0:T(8,128)(2,1)S(1)} %copy-done.62, bf16[1024,2048]{1,0:T(8,128)(2,1)} %all-gather.8.cloned.1.call-done, f32[2048]{0:T(1024)S(1)} %bitcast.389, f32[1024]{0:T(1024)S(1)} %add_rsqrt_fusion), kind=kOutput, calls=%fused_computation.12 | convolution fusion | flops 12912164864 | bytes 23080960 | tf_op jit(solution)/shard_map/dot_general | solution.py:122
  489.6 13.4 %copy.367 = bf16[4,1,256,1536]{3,2,0,1:T(8,128)(2,1)S(1)} copy(bf16[4,1,256,1536]{2,1,0,3:T(2,128)(2,1)} %get-tuple-element.200) | data formatting | bytes 6291456
  513.0 14.0 %collective-permute-done.41 = bf16[2,128,1536]{2,1,0:T(8,128)(2,1)} collective-permute-done((bf16[2,128,1536]{2,1,0:T(8,128)(2,1)}, bf16[2,128,1536]{2,1,0:T(8,128)(2,1)}, u32[]{:S(2)}, u32[]{:S(2)}) %collective-permute-start.41) | collective-permute-done | bytes 786464 | tf_op jit(solution)/shard_map/ppermute | solution.py:20
  537.2 7.4 fusion
  555.8 26.0 %collective-permute-done.36 = bf16[2,128,3072]{2,1,0:T(8,128)(2,1)} collective-permute-done((bf16[2,128,3072]{2,1,0:T(8,128)(2,1)}, bf16[2,128,3072]{2,1,0:T(8,128)(2,1)}, u32[]{:S(2)}, u32[]{:S(2)}) %collective-permute-start.36) | collective-permute-done | bytes 1572896 | tf_op jit(solution)/shard_map/ppermute | solution.py:20
  593.5 8.9 collective-permute-done.37
  604.9 29.2 %all-gather.10.cloned.1.call-done = bf16[1024,2048]{1,0:T(8,128)(2,1)} async-done(((bf16[1024,512]{1,0:T(8,128)(2,1)}), bf16[1024,2048]{1,0:T(8,128)(2,1)}) %all-gather.10.cloned.1.call-update) | async-done | bytes 4194320 | tf_op jit(solution)/shard_map/all_gather | solution.py:556
  634.1 8.2 fusion.99.grad_ref
  642.3 17.7 %reverse_scan.1 = (bf16[4,256,768]{2,1,0:T(8,128)(2,1)}, f32[4,256,768]{2,1,0:T(8,128)}, f32[4,256,768]{2,1,0:T(8,128)}, f32[4,256,768]{2,1,0:T(8,128)}) custom-call(f32[4,256,768]{2,1,0:T(8,128)} %fusion.99.grad_ref, f32[4,256,768]{2,1,0:T(8,128)} %bitcast.341, f32[4,256,768]{2,1,0:T(8,128)} %get-tuple-element.196.state_ref, ...), custom_call_target="tpu_custom_call" | custom-call | flops 31457280 | bytes 23592960 | tf_op jit(solution)/shard_map/reverse_scan/pallas_call | solution.py:302
  668.7 32.2 %gates_backward.1 = (bf16[4,256,768]{2,1,0:T(8,128)(2,1)}, f32[4,8,768]{2,1,0:T(8,128)}, f32[4,8,768]{2,1,0:T(8,128)}, f32[64,768]{1,0:T(8,128)}, f32[768,1536]{1,0:T(8,128)}) custom-call(f32[4,256,768]{2,1,0:T(8,128)} %get-tuple-element.35.direct_ref, f32[4,256,768]{2,1,0:T(8,128)} %get-tuple-element.36.coef_ref, ...), custom_call_target="tpu_custom_call" | custom-call | flops 4831838208 | bytes 26738688 | tf_op jit(solution)/shard_map/gates_backward/pallas_call | solution.py:413
  717.1 8.4 convolution_convert_fusion.2
  731.5 11.6 %fusion.8 = (f32[2048]{0:T(1024)S(1)}, f32[1024]{0:T(1024)S(1)}, f32[1024,2048]{1,0:T(8,128)}) fusion(bf16[1024,2048]{1,0:T(8,128)(2,1)S(1)} %copy-done.1, f32[1024]{0:T(1024)S(1)} %copy-done.55, f32[2048]{0:T(1024)S(1)} %bitcast.384, bf16[2048,1536]{1,0:T(8,128)(2,1)} %bitcast.8, bf16[1024,768]{1,0:T(8,128)(2,1)S(1)} %bitcast.398, ...), kind=kOutput, calls=%fused_computation.20 | convolution fusion | flops 6463419392 | bytes 22044672 | tf_op jit(solution)/shard_map/dot_general | solution.py:118
  744.8 24.9 %reduce-scatter.16.cloned.1.call-done = f32[512,2]{1,0:T(8,128)} async-done(((f32[2048,2]{1,0:T(8,128)}), f32[512,2]{1,0:T(8,128)}) %reduce-scatter.16.cloned.1.call-update) | async-done | bytes 4112
  795.4 25.7 %collective-permute-done.31 = bf16[2,128,768]{2,1,0:T(8,128)(2,1)S(1)} collective-permute-done((bf16[2,128,768]{2,1,0:T(8,128)(2,1)S(1)}, bf16[2,128,768]{2,1,0:T(8,128)(2,1)S(1)}, u32[]{:S(2)}, u32[]{:S(2)}) %collective-permute-start.31) | collective-permute-done | bytes 393248 | tf_op jit(solution)/shard_map/ppermute | solution.py:20
  835.5 15.2 %collective-permute-done.47 = f32[4,176,352]{2,1,0:T(8,128)} collective-permute-done((f32[4,176,352]{2,1,0:T(8,128)}, f32[4,176,352]{2,1,0:T(8,128)}, u32[]{:S(2)}, u32[]{:S(2)}) %collective-permute-start.47) | collective-permute-done | bytes 991264 | tf_op jit(solution)/shard_map/ppermute | solution.py:20
  857.2 15.7 %collective-permute-done.28 = bf16[2,128,1536]{2,1,0:T(8,128)(2,1)S(1)} collective-permute-done((bf16[2,128,1536]{2,1,0:T(8,128)(2,1)S(1)}, bf16[2,128,1536]{2,1,0:T(8,128)(2,1)S(1)}, u32[]{:S(2)}, u32[]{:S(2)}) %collective-permute-start.28) | collective-permute-done | bytes 786464 | tf_op jit(solution)/shard_map/ppermute | solution.py:20
  (439 shorter events, 343.3 us)
Async XLA Ops:
  7.2 98.2 %all-gather.6.cloned.1.call-start = ((), (), s32[]{:S(2)}) async-start(), calls=%async_computation.5 | async-start | bytes 5242880 | tf_op jit(solution)/shard_map/all_gather | solution.py:481
  9.4 20.7 %collective-permute-start = (bf16[256,1536]{0,1:T(8,128)(2,1)}, bf16[256,1536]{0,1:T(8,128)(2,1)}, u32[]{:S(2)}, u32[]{:S(2)}) collective-permute-start(bf16[256,1536]{0,1:T(8,128)(2,1)} %get-tuple-element.224), channel_id=1, source_target_pairs={{0,16},{16,0},{1,17},{17,1},{2,18},{18,2},{3,19},{19,3},{4,20},{20... | collective-permute-start | bytes 2359304 | tf_op jit(solution)/shard_map/ppermute | solution.py:20
  9.9 22.5 %collective-permute-start.1 = (bf16[256,1536]{0,1:T(8,128)(2,1)}, bf16[256,1536]{0,1:T(8,128)(2,1)}, u32[]{:S(2)}, u32[]{:S(2)}) collective-permute-start(bf16[256,1536]{0,1:T(8,128)(2,1)} %get-tuple-element.224), channel_id=1, source_target_pairs={{0,8},{4,12},{8,0},{12,4},{1,9},{5,13},{9,1},{13,5},{2,10},{6,14},... | collective-permute-start | bytes 2359304 | tf_op jit(solution)/shard_map/ppermute | solution.py:20
  13.4 68.6 %collective-permute-start.6 = (bf16[256,768]{1,0:T(8,128)(2,1)}, bf16[256,768]{1,0:T(8,128)(2,1)}, u32[]{:S(2)}, u32[]{:S(2)}) collective-permute-start(bf16[256,768]{1,0:T(8,128)(2,1)} %pad.85), channel_id=1, source_target_pairs={{0,16},{16,0},{1,17},{17,1},{2,18},{18,2},{3,19},{19,3},{4,20},{20... | collective-permute-start | bytes 1179656 | tf_op jit(solution)/shard_map/ppermute | solution.py:20
  14.9 65.5 %collective-permute-start.7 = (bf16[256,768]{1,0:T(8,128)(2,1)}, bf16[256,768]{1,0:T(8,128)(2,1)}, u32[]{:S(2)}, u32[]{:S(2)}) collective-permute-start(bf16[256,768]{1,0:T(8,128)(2,1)} %pad.85), channel_id=1, source_target_pairs={{0,8},{4,12},{8,0},{12,4},{1,9},{5,13},{9,1},{13,5},{2,10},{6,14},... | collective-permute-start | bytes 1179656 | tf_op jit(solution)/shard_map/ppermute | solution.py:20
  15.4 232.4 %reduce-scatter.8.cloned.1.call-start = ((), (), s32[]{:S(2)}) async-start(), calls=%async_computation.6 | async-start | bytes 5242880 | tf_op jit(solution)/shard_map/reduce_scatter | solution.py:532
  52.4 47.6 %collective-permute-start.4 = (bf16[4,1,256,1536]{3,2,1,0:T(8,128)(2,1)S(1)}, bf16[4,1,256,1536]{3,2,1,0:T(8,128)(2,1)}, u32[]{:S(2)}, u32[]{:S(2)}) collective-permute-start(bf16[4,1,256,1536]{3,2,1,0:T(8,128)(2,1)S(1)} %bitcast.342), channel_id=1, source_target_pairs={{0,4},{4,0},{8,12},{12,8},{1,5},{5,1},{9,13},{13,9},{2,6},{6,2},{1... | collective-permute-start | bytes 9437192 | tf_op jit(solution)/shard_map/ppermute | solution.py:20
  170.8 158.5 %all-gather.8.cloned.1.call-start = ((), (), s32[]{:S(2)}) async-start(), calls=%async_computation.7 | async-start | bytes 5242880 | tf_op jit(solution)/shard_map/all_gather | solution.py:534
  172.3 36.7 %collective-permute-start.12 = (bf16[256,3072]{1,0:T(8,128)(2,1)S(1)}, bf16[256,3072]{1,0:T(8,128)(2,1)S(1)}, u32[]{:S(2)}, u32[]{:S(2)}) collective-permute-start(bf16[256,3072]{1,0:T(8,128)(2,1)S(1)} %constant_dynamic-update-slice_fusion), channel_id=1, source_target_pairs={{0,8},{4,12},{8,0},{12,4},{1,9},{5,13},{9,1},{13,5},{2,10},{6,14},... | collective-permute-start | bytes 4718600 | tf_op jit(solution)/shard_map/ppermute | solution.py:20
  173.8 36.8 %collective-permute-start.11 = (bf16[256,3072]{1,0:T(8,128)(2,1)S(1)}, bf16[256,3072]{1,0:T(8,128)(2,1)S(1)}, u32[]{:S(2)}, u32[]{:S(2)}) collective-permute-start(bf16[256,3072]{1,0:T(8,128)(2,1)S(1)} %constant_dynamic-update-slice_fusion), channel_id=1, source_target_pairs={{0,16},{16,0},{1,17},{17,1},{2,18},{18,2},{3,19},{19,3},{4,20},{20... | collective-permute-start | bytes 4718600 | tf_op jit(solution)/shard_map/ppermute | solution.py:20
  230.5 80.0 %collective-permute-start.15 = (bf16[4,1,256,3072]{3,2,1,0:T(8,128)(2,1)}, bf16[4,1,256,3072]{3,2,1,0:T(8,128)(2,1)}, u32[]{:S(2)}, u32[]{:S(2)}) collective-permute-start(bf16[4,1,256,3072]{3,2,1,0:T(8,128)(2,1)} %bitcast.47), channel_id=1, source_target_pairs={{0,4},{4,0},{8,12},{12,8},{1,5},{5,1},{9,13},{13,9},{2,6},{6,2},{1... | collective-permute-start | bytes 18874376 | tf_op jit(solution)/shard_map/ppermute | solution.py:20
  250.3 283.9 %reduce-scatter.12.cloned.1.call-start = ((), (), s32[]{:S(2)}) async-start(), calls=%async_computation.9 | async-start | bytes 5242880 | tf_op jit(solution)/shard_map/reduce_scatter | solution.py:552
  251.5 21.4 %collective-permute-start.17 = (bf16[256,1536]{0,1:T(8,128)(2,1)}, bf16[256,1536]{0,1:T(8,128)(2,1)}, u32[]{:S(2)}, u32[]{:S(2)}) collective-permute-start(bf16[256,1536]{0,1:T(8,128)(2,1)} %bitcast.49), channel_id=1, source_target_pairs={{0,8},{4,12},{8,0},{12,4},{1,9},{5,13},{9,1},{13,5},{2,10},{6,14},... | collective-permute-start | bytes 2359304 | tf_op jit(solution)/shard_map/ppermute | solution.py:20
  396.4 194.1 %reduce-scatter.10.cloned.1.call-start = ((), (), s32[]{:S(2)}) async-start(), calls=%async_computation.8 | async-start | bytes 5242880 | tf_op jit(solution)/shard_map/reduce_scatter | solution.py:561
  450.0 53.0 %collective-permute-start.40 = (bf16[4,256,1536]{2,1,0:T(8,128)(2,1)}, bf16[4,256,1536]{2,1,0:T(8,128)(2,1)}, u32[]{:S(2)}, u32[]{:S(2)}) collective-permute-start(bf16[4,256,1536]{2,1,0:T(8,128)(2,1)} %bitcast.120), channel_id=1, source_target_pairs={{0,4},{4,0},{8,12},{12,8},{1,5},{5,1},{9,13},{13,9},{2,6},{6,2},{1... | collective-permute-start | bytes 9437192 | tf_op jit(solution)/shard_map/ppermute | solution.py:20
  461.1 173.0 %all-gather.10.cloned.1.call-start = ((), (), s32[]{:S(2)}) async-start(), calls=%async_computation.10 | async-start | bytes 5242880 | tf_op jit(solution)/shard_map/all_gather | solution.py:556
  489.2 48.0 %collective-permute-start.35 = (bf16[4,256,3072]{2,1,0:T(8,128)(2,1)}, bf16[4,256,3072]{2,1,0:T(8,128)(2,1)}, u32[]{:S(2)}, u32[]{:S(2)}) collective-permute-start(bf16[4,256,3072]{2,1,0:T(8,128)(2,1)} %dynamic-slice_bitcast_fusion), channel_id=1, source_target_pairs={{0,4},{4,0},{8,12},{12,8},{1,5},{5,1},{9,13},{13,9},{2,6},{6,2},{1... | collective-permute-start | bytes 18874376 | tf_op jit(solution)/shard_map/ppermute | solution.py:20
  508.5 22.2 %collective-permute-start.43 = (bf16[2,128,1536]{2,1,0:T(8,128)(2,1)}, bf16[2,128,1536]{2,1,0:T(8,128)(2,1)}, u32[]{:S(2)}, u32[]{:S(2)}) collective-permute-start(bf16[2,128,1536]{2,1,0:T(8,128)(2,1)} %dynamic-slice_bitcast_fusion.5), channel_id=1, source_target_pairs={{0,8},{4,12},{8,0},{12,4},{1,9},{5,13},{9,1},{13,5},{2,10},{6,14},... | collective-permute-start | bytes 2359304 | tf_op jit(solution)/shard_map/ppermute | solution.py:20
  537.0 232.7 %reduce-scatter.16.cloned.1.call-start = ((), (), s32[]{:S(2)}) async-start(), calls=%async_computation.12 | async-start | bytes 1310720
  546.4 35.4 %collective-permute-start.36 = (bf16[2,128,3072]{2,1,0:T(8,128)(2,1)}, bf16[2,128,3072]{2,1,0:T(8,128)(2,1)}, u32[]{:S(2)}, u32[]{:S(2)}) collective-permute-start(bf16[2,128,3072]{2,1,0:T(8,128)(2,1)} %dynamic-slice_bitcast_fusion.3), channel_id=1, source_target_pairs={{0,16},{16,0},{1,17},{17,1},{2,18},{18,2},{3,19},{19,3},{4,20},{20... | collective-permute-start | bytes 4718600 | tf_op jit(solution)/shard_map/ppermute | solution.py:20
  550.5 36.0 %collective-permute-start.38 = (bf16[2,128,3072]{2,1,0:T(8,128)(2,1)}, bf16[2,128,3072]{2,1,0:T(8,128)(2,1)}, u32[]{:S(2)}, u32[]{:S(2)}) collective-permute-start(bf16[2,128,3072]{2,1,0:T(8,128)(2,1)} %dynamic-slice_bitcast_fusion.2), channel_id=1, source_target_pairs={{0,8},{4,12},{8,0},{12,4},{1,9},{5,13},{9,1},{13,5},{2,10},{6,14},... | collective-permute-start | bytes 4718600 | tf_op jit(solution)/shard_map/ppermute | solution.py:20
  589.6 188.9 %collective-permute-start.39 = (bf16[128,3072]{1,0:T(8,128)(2,1)}, bf16[128,3072]{1,0:T(8,128)(2,1)}, u32[]{:S(2)}, u32[]{:S(2)}) collective-permute-start(bf16[128,3072]{1,0:T(8,128)(2,1)} %dynamic-slice_bitcast_fusion.7), channel_id=1, source_target_pairs={{0,16},{16,0},{1,17},{17,1},{2,18},{18,2},{3,19},{19,3},{4,20},{20... | collective-permute-start | bytes 2359304 | tf_op jit(solution)/shard_map/ppermute | solution.py:20
  704.0 82.2 %collective-permute-start.45 = (f32[4,176,352]{2,1,0:T(8,128)}, f32[4,176,352]{2,1,0:T(8,128)}, u32[]{:S(2)}, u32[]{:S(2)}) collective-permute-start(f32[4,176,352]{2,1,0:T(8,128)} %maximum_maximum_fusion), channel_id=1, source_target_pairs={{0,4},{4,0},{8,12},{12,8},{1,5},{5,1},{9,13},{13,9},{2,6},{6,2},{1... | collective-permute-start | bytes 2973704 | tf_op jit(solution)/shard_map/ppermute | solution.py:20
  711.6 77.1 %collective-permute-start.30 = (bf16[4,256,768]{2,1,0:T(8,128)(2,1)}, bf16[4,256,768]{2,1,0:T(8,128)(2,1)}, u32[]{:S(2)}, u32[]{:S(2)}) collective-permute-start(bf16[4,256,768]{2,1,0:T(8,128)(2,1)} %dynamic-slice_bitcast_fusion.4), channel_id=1, source_target_pairs={{0,4},{4,0},{8,12},{12,8},{1,5},{5,1},{9,13},{13,9},{2,6},{6,2},{1... | collective-permute-start | bytes 4718600 | tf_op jit(solution)/shard_map/ppermute | solution.py:20
  729.2 98.3 %collective-permute-start.25 = (bf16[4,256,1536]{2,1,0:T(8,128)(2,1)}, bf16[4,256,1536]{2,1,0:T(8,128)(2,1)}, u32[]{:S(2)}, u32[]{:S(2)}) collective-permute-start(bf16[4,256,1536]{2,1,0:T(8,128)(2,1)} %dynamic-slice_bitcast_fusion.1), channel_id=1, source_target_pairs={{0,4},{4,0},{8,12},{12,8},{1,5},{5,1},{9,13},{13,9},{2,6},{6,2},{1... | collective-permute-start | bytes 9437192 | tf_op jit(solution)/shard_map/ppermute | solution.py:20
  744.5 139.0 %reduce-scatter.14.cloned.1.call-start = ((), (), s32[]{:S(2)}) async-start(), calls=%async_computation.11 | async-start | bytes 5242880 | tf_op jit(solution)/shard_map/reduce_scatter | solution.py:587
  788.1 35.8 %collective-permute-start.46 = (f32[4,176,352]{2,1,0:T(8,128)S(1)}, f32[4,176,352]{2,1,0:T(8,128)S(1)}, u32[]{:S(2)}, u32[]{:S(2)}) collective-permute-start(f32[4,176,352]{2,1,0:T(8,128)S(1)} %fusion.115), channel_id=1, source_target_pairs={{0,16},{16,0},{1,17},{17,1},{2,18},{18,2},{3,19},{19,3},{4,20},{20... | collective-permute-start | bytes 2973704 | tf_op jit(solution)/shard_map/ppermute | solution.py:20
  790.9 30.3 %collective-permute-start.31 = (bf16[2,128,768]{2,1,0:T(8,128)(2,1)S(1)}, bf16[2,128,768]{2,1,0:T(8,128)(2,1)S(1)}, u32[]{:S(2)}, u32[]{:S(2)}) collective-permute-start(bf16[2,128,768]{2,1,0:T(8,128)(2,1)S(1)} %dynamic-slice_bitcast_fusion.14), channel_id=1, source_target_pairs={{0,16},{16,0},{1,17},{17,1},{2,18},{18,2},{3,19},{19,3},{4,20},{20... | collective-permute-start | bytes 1179656 | tf_op jit(solution)/shard_map/ppermute | solution.py:20
  793.0 30.1 %collective-permute-start.33 = (bf16[2,128,768]{2,1,0:T(8,128)(2,1)S(1)}, bf16[2,128,768]{2,1,0:T(8,128)(2,1)S(1)}, u32[]{:S(2)}, u32[]{:S(2)}) collective-permute-start(bf16[2,128,768]{2,1,0:T(8,128)(2,1)S(1)} %dynamic-slice_bitcast_fusion.13), channel_id=1, source_target_pairs={{0,8},{4,12},{8,0},{12,4},{1,9},{5,13},{9,1},{13,5},{2,10},{6,14},... | collective-permute-start | bytes 1179656 | tf_op jit(solution)/shard_map/ppermute | solution.py:20
  826.4 24.2 %collective-permute-start.47 = (f32[4,176,352]{2,1,0:T(8,128)}, f32[4,176,352]{2,1,0:T(8,128)}, u32[]{:S(2)}, u32[]{:S(2)}) collective-permute-start(f32[4,176,352]{2,1,0:T(8,128)} %fusion.116), channel_id=1, source_target_pairs={{0,8},{4,12},{8,0},{12,4},{1,9},{5,13},{9,1},{13,5},{2,10},{6,14},... | collective-permute-start | bytes 2973704 | tf_op jit(solution)/shard_map/ppermute | solution.py:20
  831.6 23.6 %collective-permute-start.26 = (bf16[2,128,1536]{2,1,0:T(8,128)(2,1)}, bf16[2,128,1536]{2,1,0:T(8,128)(2,1)}, u32[]{:S(2)}, u32[]{:S(2)}) collective-permute-start(bf16[2,128,1536]{2,1,0:T(8,128)(2,1)} %dynamic-slice_bitcast_fusion.10), channel_id=1, source_target_pairs={{0,16},{16,0},{1,17},{17,1},{2,18},{18,2},{3,19},{19,3},{4,20},{20... | collective-permute-start | bytes 2359304 | tf_op jit(solution)/shard_map/ppermute | solution.py:20
  856.6 21.9 %collective-permute-start.27 = (bf16[128,1536]{1,0:T(8,128)(2,1)S(1)}, bf16[128,1536]{1,0:T(8,128)(2,1)S(1)}, u32[]{:S(2)}, u32[]{:S(2)}) collective-permute-start(bf16[128,1536]{1,0:T(8,128)(2,1)S(1)} %dynamic-slice_bitcast_fusion.16), channel_id=1, source_target_pairs={{0,8},{4,12},{8,0},{12,4},{1,9},{5,13},{9,1},{13,5},{2,10},{6,14},... | collective-permute-start | bytes 1179656 | tf_op jit(solution)/shard_map/ppermute | solution.py:20
  (89 other events, 991.5 us)
Sparse Core Ops, SparseCore 0:
  15.6 79.5 all-gather.5
  171.0 76.7 reduce-scatter.7
  250.4 78.8 all-gather.7
  396.5 77.7 reduce-scatter.11
  476.4 77.2 reduce-scatter.9
  555.2 78.8 all-gather.9
  744.6 25.1 reduce-scatter.15
  777.9 77.5 reduce-scatter.13

commit v2 on v1

--- a/solution.py
+++ b/solution.py
@@ -1,9 +1,8 @@
-import functools
-
 import jax
 import jax.numpy as jnp
 from jax import lax
 from jax.experimental import pallas as pl
+from jax.experimental.layout import Layout, with_layout_constraint
 from jax.experimental.pallas import tpu as pltpu
 from jax.sharding import PartitionSpec as P
 
@@ -37,24 +36,44 @@
     own_x, own_y, own_c = own_place()
     from_x = xor_permute(shard, "fsdp", 1)
     from_y = xor_permute(shard, "ctx", 2)
-    corner_top = xor_permute(from_y[:half], "fsdp", 1)
-    corner_low = xor_permute(from_x[half:], "ctx", 2)
-    quad = jnp.zeros((2, 2, rows, width), shard.dtype)
-
-    def place(buffer, block, at_x, at_y, row):
-        return lax.dynamic_update_slice(buffer, block[None, None], (at_x, at_y, row, 0))
-
-    quad = place(quad, shard, own_x, own_y, 0)
-    quad = place(quad, from_x, 1 - own_x, own_y, 0)
-    quad = place(quad, from_y, own_x, 1 - own_y, 0)
-    quad = place(quad, corner_top, 1 - own_x, 1 - own_y, 0)
-    quad = place(quad, corner_low, 1 - own_x, 1 - own_y, half)
-    quad = quad.reshape(4, 1, rows, width)
+    corner = jnp.concatenate(
+        [xor_permute(from_y[:half], "fsdp", 1), xor_permute(from_x[half:], "ctx", 2)], axis=0
+    )
+    quad = [
+        jnp.where(
+            own_x == x, jnp.where(own_y == y, shard, from_y), jnp.where(own_y == y, from_x, corner)
+        )
+        for x in range(2)
+        for y in range(2)
+    ]
+    quad = jnp.concatenate(quad, axis=0).reshape(4, 1, rows, width)
     other = xor_permute(quad, "ctx", 1)
     full = jnp.zeros((4, 2, rows, width), shard.dtype)
     full = lax.dynamic_update_slice(full, quad, (0, own_c, 0, 0))
     full = lax.dynamic_update_slice(full, other, (0, 1 - own_c, 0, 0))
     return full.reshape(8 * rows, width)
+
+
+def row_major(value):
+    return with_layout_constraint(value, Layout(major_to_minor=tuple(range(value.ndim))))
+
+
+def choose(options, index):
+    value = options[0]
+    for position, option in enumerate(options[1:], 1):
+        value = jnp.where(index == position, option, value)
+    return value
+
+
+def shifted_permute(value, step):
+    count = lax.axis_size("tp")
+    return lax.ppermute(value, "tp", [(i, (i + step) % count) for i in range(count)])
+
+
+def exchange(block_for):
+    count, mine = lax.axis_size("tp"), lax.axis_index("tp")
+    got = [shifted_permute(block_for(step), step) if step else block_for(0) for step in range(count)]
+    return [choose([got[(at - source) % count] for at in range(count)], mine) for source in range(count)]
 
 
 def pick(value, index, axis):
@@ -282,7 +301,7 @@
     def body(at):
         window = pl.ds(at, 32)
         act, slope = gelu_parts(y_ref[window, :])
-        grad = grad_ref[window, :]
+        grad = grad_ref[window, :].astype(F32)
         y_grad_ref[window, :] = (grad * state_ref[window, :] * slope).astype(BF16)
         direct = grad * act
         coef = jnp.exp(decay * rate_ref[window, :]) * mask_ref[window, 1:2]
@@ -470,6 +489,8 @@
     hidden_width = gate_proj.shape[1]
     heads, size, _ = rate_gate.shape
     padded = -(-rec_width // LANES) * LANES
+    group = lax.axis_size("tp")
+    own_rows = row_count // group
     extra = padded - rec_width
 
     def widen(value):
@@ -483,10 +504,11 @@
     gain_one, gain_two = gains[0:1], gains[1:2]
     full_width = x_full.shape[1]
 
-    w_in = gather_rows(jnp.concatenate([widen(gelu_proj), widen(scan_proj)], axis=1))
-    w_out = gather_rows(widen(out_proj.T))
+    w_in = gather_rows(row_major(jnp.concatenate([widen(gelu_proj), widen(scan_proj)], axis=1)))
+    w_down = gather_rows(row_major(down_proj.T))
+    x_full, out_shard = lax.optimization_barrier((x_full, row_major(widen(out_proj.T))))
+    w_out = gather_rows(jnp.concatenate(exchange(lambda step: out_shard), axis=1))
     w_ff = gather_rows(jnp.concatenate([gate_proj, up_proj], axis=1))
-    w_down = gather_rows(down_proj.T)
 
     margin = CONV - 1
     start_tok = lax.axis_index("ctx") * tok_count
@@ -526,14 +548,22 @@
     state_in = entering(coef[:, -1], local[:, -1], False)
     states = local + coef * state_in[:, None, :]
     y_act, _ = gelu_parts(y_pre)
-    mixed_in = (states * y_act).astype(BF16).reshape(row_count, padded)
-
-    rec_part = dot_nt(mixed_in, w_out).astype(BF16)
-    rec_own = lax.psum_scatter(rec_part, "tp", scatter_dimension=1, tiled=True)
-    mid_own = block_in.reshape(row_count, part_width).astype(F32) + rec_own.astype(F32)
-    mid = lax.all_gather(mid_own.astype(BF16), "tp", axis=1, tiled=True).astype(F32)
+    mixed_in = (states * y_act).astype(BF16).reshape(group, own_rows, padded)
+
+    mine = lax.axis_index("tp")
+    mixed = jnp.concatenate(
+        exchange(lambda step: pick(mixed_in, lax.rem(mine + step, group), 0)), axis=1
+    )
+    own = lambda value: lax.dynamic_slice_in_dim(value, mine * own_rows, own_rows, 0)
+    x_own = own(x_full).astype(F32)
+    mid = x_own + dot_nt(mixed, w_out)
     scale_two = lax.rsqrt(jnp.mean(mid * mid, axis=-1, keepdims=True) + EPS)
-    normed_mid = (mid * scale_two * gain_two).astype(BF16)
+    normed_mid = lax.all_gather((mid * scale_two * gain_two).astype(BF16), "tp", axis=0, tiled=True)
+    here = (jnp.arange(group) == mine).astype(F32)[:, None, None]
+
+    def with_own(part, value):
+        total = part.reshape(group, own_rows, full_width) + here * value[None]
+        return total.astype(BF16).reshape(row_count, full_width)
 
     cot = out_cot.reshape(row_count, full_width)
     hid_grad = dot_nn(cot, w_down)
@@ -544,25 +574,35 @@
     both_grad = jnp.concatenate(
         [(hid_grad * up_pre * gate_slope).astype(BF16), (hid_grad * gate_act).astype(BF16)], axis=1
     )
-    mid_part = dot_nt(both_grad, w_ff)
-    weighted = mid_part * gain_two
+    mid_part = dot_nt(both_grad, w_ff).astype(BF16)
+    mid_norm_grad = lax.psum_scatter(mid_part, "tp", scatter_dimension=0, tiled=True)
+    mlp_part = with_own(dot_nt(hidden, w_down), mid)
+    mid_norm_grad, mlp_part = lax.optimization_barrier((mid_norm_grad, mlp_part))
+    block_out = split(lax.psum_scatter(mlp_part, "tp", scatter_dimension=1, tiled=True))
+
+    mid_norm_grad = mid_norm_grad.astype(F32)
+    weighted = mid_norm_grad * gain_two
     mean_two = jnp.mean(weighted * mid, axis=-1, keepdims=True)
-    back_two = (scale_two * weighted - mid * (scale_two * scale_two * scale_two * mean_two)).astype(BF16)
-    gain_two_part = jnp.sum(mid_part * mid * scale_two, axis=0)
-    back_own = lax.psum_scatter(back_two, "tp", scatter_dimension=1, tiled=True)
-    col_start = lax.axis_index("tp") * part_width
-    cot_own = lax.dynamic_slice_in_dim(cot, col_start, part_width, 1).astype(F32)
-    mid_grad_own = cot_own + back_own.astype(F32)
-    rec_grad = lax.all_gather(mid_grad_own.astype(BF16), "tp", axis=1, tiled=True)
-
-    mlp_part = dot_nt(hidden, w_down).astype(BF16)
-    grad_down = scatter_rows(dot_tn(cot, hidden).astype(BF16))
+    mid_grad = (
+        own(cot).astype(F32)
+        + scale_two * weighted
+        - mid * (scale_two * scale_two * scale_two * mean_two)
+    )
+    gain_two_part = jnp.sum(mid_norm_grad * mid * scale_two, axis=0)
+    rec_grad = mid_grad.astype(BF16)
+    mixed_grad_own = dot_nn(rec_grad, w_out).astype(BF16)
+    by_heads = [mixed_grad_own[:, g * padded : (g + 1) * padded] for g in range(group)]
+    mixed_grad = exchange(lambda step: choose(by_heads[step:] + by_heads[:step], mine))
+    mixed_grad = split(jnp.concatenate(mixed_grad, axis=0))
+
+    grad_down = scatter_rows(row_major(dot_tn(cot, hidden).astype(BF16)))
     grad_ff = scatter_rows(dot_tn(normed_mid, both_grad).astype(BF16))
-    mlp_own = lax.psum_scatter(mlp_part, "tp", scatter_dimension=1, tiled=True)
-    block_out = split((mid_own + mlp_own.astype(F32)).astype(BF16))
-
-    mixed_grad = split(dot_nn(rec_grad, w_out))
-    grad_out = scatter_rows(dot_tn(rec_grad, mixed_in).astype(BF16))
+    grad_out = scatter_rows(dot_tn(rec_grad, mixed).astype(BF16)).astype(BF16)
+    by_heads_out = [grad_out[:, g * padded : (g + 1) * padded] for g in range(group)]
+    grad_out = sum(
+        part.astype(F32) for part in exchange(lambda step: choose(by_heads_out[step:] + by_heads_out[:step], mine))
+    )
+
     y_grad, direct, tail_coef, tail_value = reverse_call(mixed_grad, y_pre, states, rate, back, vectors)
     enter = entering(tail_coef[:, 0], tail_value[:, 0], True)
     rows_of = lambda value: jnp.broadcast_to(value[:, None, :], (seq_count, 8, padded))
@@ -582,15 +622,15 @@
     in_part = dot_nt(in_grad, w_in)
     weighted = in_part * gain_one
     mean_one = jnp.mean(weighted * x_rows, axis=-1, keepdims=True)
-    back_one = (scale_one * weighted - x_rows * (scale_one * scale_one * scale_one * mean_one)).astype(BF16)
+    back_one = scale_one * weighted - x_rows * (scale_one * scale_one * scale_one * mean_one)
     gain_one_part = jnp.sum(in_part * x_rows * scale_one, axis=0)
-    in_own = lax.psum_scatter(back_one, "tp", scatter_dimension=1, tiled=True)
-    grad_in = split(mid_grad_own + in_own.astype(F32))
-    grad_in_w = scatter_rows(dot_tn(normed, in_grad).astype(BF16))
-
-    gain_parts = lax.psum_scatter(
-        jnp.stack([gain_one_part, gain_two_part]), "tp", scatter_dimension=1, tiled=True
-    )
+    in_total = lax.psum_scatter(with_own(back_one, mid_grad), "tp", scatter_dimension=1, tiled=True)
+    grad_in = split(in_total.astype(F32))
+    grad_in_w = scatter_rows(row_major(dot_tn(normed, in_grad).astype(BF16)))
+
+    gain_parts = jnp.stack([gain_one_part, gain_two_part])
+    by_features = [gain_parts[:, g * part_width : (g + 1) * part_width] for g in range(group)]
+    gain_parts = sum(exchange(lambda step: choose(by_features[step:] + by_features[:step], mine)))
     sums = sums.reshape(8, 8, padded).sum(axis=1)
     gain_parts = jnp.pad(gain_parts, ((0, 0), (0, padded - part_width)))
     small = total_over_tokens(jnp.concatenate([sums, gain_parts], axis=0))

time: 909 us -> 990 us (1.089)
  waiting for transfers between devices: 281 us -> 416 us
  local copies, waits for them, and re-layouts: 213 us -> 139 us
  starting transfers between devices: 47.4 us -> 68.2 us
    ppermute x0 -> x15, waiting for transfers between devices: none -> 95.9 us  [shifted_permute(): lax.ppermute(value, 'tp', [(i, (i + step) % count) for i in range(count)])]
    all_gather x1, waiting for transfers between devices: 0.01 us -> 50.8 us  [shards(): lax.all_gather(block_in.reshape(row_count, part_width), 'tp', axis=1, til...]
    unnamed x148 -> x193, local copies, waits for them, and re-layouts: 55.5 us -> 24.2 us
    broadcast_in_dim x14 -> x0, local copies, waits for them, and re-layouts: 29.6 us -> none  [the longest x10 19.5 us: place(): block[None, None]]
    unnamed x9 -> x5, waiting for transfers between devices: 25.1 us -> 0.74 us
    ppermute x46, waiting for transfers between devices: 195 us -> 219 us  [xor_permute(): return lax.ppermute(value, axis, [(i, i ^ bit) for i in range(count)])]
    ppermute x0 -> x15, starting transfers between devices: none -> 23.2 us  [shifted_permute(): lax.ppermute(value, 'tp', [(i, (i + step) % count) for i in range(count)])]
    convert_element_type x6 -> x4, other arithmetic: 28.1 us -> 11.2 us  [the longest x1 5.88 us: shards(): mixed_in = (states * y_act).astype(BF16).reshape(group, own_rows, padded)]
  transfers between devices with their start and end apart: 56 -> 68, of which waited for: 27 -> 35; matrix products, arithmetic and copies ran while one was open for 38% -> 32% of each run, Pallas kernels for 6% -> 8%
where the time goes in v2:
time: 990 us; the launch traced here: 980 us
  waiting for transfers between devices  416 us (42%)
  matrix products  149 us (15%)
  local copies, waits for them, and re-layouts  139 us (14%)
  other arithmetic  90.1 us (9%)
  Pallas kernels  77.6 us (8%)
  starting transfers between devices  68.2 us (7%)
  blocking collectives  23.2 us (2%)
  between operations  16 us (2%)
    ppermute x46, waiting for transfers between devices, xor_permute(): return lax.ppermute(value, axis, [(i, i ^ bit) for i in range(count)])  219 us
    ppermute x15, waiting for transfers between devices, shifted_permute(): lax.ppermute(value, 'tp', [(i, (i + step) % count) for i in range(count)])  95.9 us
    dot_general x5, matrix products, dot_nn(): return jnp.dot(left, right, preferred_element_type=F32)  53.1 us
    all_gather x1, waiting for transfers between devices, shards(): lax.all_gather(block_in.reshape(row_count, part_width), 'tp', axis=1, til...  50.8 us
    dot_general x4, matrix products, dot_nt(): lax.dot_general(left, right, (((1,), (1,)), ((), ())), preferred_element_...  50.4 us
    dot_general x4, matrix products, dot_tn(): lax.dot_general(left, right, (((0,), (0,)), ((), ())), preferred_element_...  45.7 us
    ppermute x46, starting transfers between devices, xor_permute(): return lax.ppermute(value, axis, [(i, i ^ bit) for i in range(count)])  40.2 us
    all_gather x1, waiting for transfers between devices, shards(): lax.all_gather((mid * scale_two * gain_two).astype(BF16), 'tp', axis=0, t...  36.6 us
  transfers between devices with their start and end apart: 68, of which 35 were waited for; matrix products, arithmetic and copies ran while one was open for 32% of the time, Pallas kernels for 8%

profile of v2, /device:TPU:10, one launch (start us, length us, event | category | flops | bytes accessed | tf_op | source)
XLA Modules:
  0.0 979.7 jit_solution(5443983465349862161)
XLA Ops:
  19.3 12.4 %all_gather.22 = bf16[2,2048]{1,0:T(2,128)(2,1)S(1)} all-gather(bf16[2,512]{1,0:T(2,128)(2,1)S(1)} %pad_maximum_fusion.24), channel_id=1, replica_groups=mesh['fsdp'=2,'ctx'=4,'tp'=4] {'tp'}, dimensions={1}, use_global_device_ids=true | all-gather | bytes 10240 | tf_op jit(solution)/shard_map/all_gather | solution.py:503
  38.5 50.8 %all-gather.5.cloned.1.call-done = bf16[1024,2048]{1,0:T(8,128)(2,1)} async-done(((bf16[1024,512]{1,0:T(8,128)(2,1)}), bf16[1024,2048]{1,0:T(8,128)(2,1)}) %all-gather.5.cloned.1.call-update) | async-done | bytes 4194320 | tf_op jit(solution)/shard_map/all_gather | solution.py:502
  103.5 14.6 %collective-permute-done.15 = bf16[256,768]{1,0:T(8,128)(2,1)S(1)} collective-permute-done((bf16[256,768]{1,0:T(8,128)(2,1)S(1)}, bf16[256,768]{1,0:T(8,128)(2,1)S(1)}, u32[]{:S(2)}, u32[]{:S(2)}) %collective-permute-start.15) | collective-permute-done | bytes 393248 | tf_op jit(solution)/shard_map/ppermute | solution.py:70
  154.8 19.7 %collective-permute-done.17 = bf16[256,3072]{1,0:T(8,128)(2,1)S(1)} collective-permute-done((bf16[256,3072]{1,0:T(8,128)(2,1)}, bf16[256,3072]{1,0:T(8,128)(2,1)S(1)}, u32[]{:S(2)}, u32[]{:S(2)}) %collective-permute-start.17) | collective-permute-done | bytes 1572896 | tf_op jit(solution)/shard_map/ppermute | solution.py:19
  183.0 16.8 %collective-permute-done.24 = bf16[128,3072]{1,0:T(8,128)(2,1)S(1)} collective-permute-done((bf16[128,3072]{1,0:T(8,128)(2,1)S(1)}, bf16[128,3072]{1,0:T(8,128)(2,1)S(1)}, u32[]{:S(2)}, u32[]{:S(2)}) %collective-permute-start.24) | collective-permute-done | bytes 786464 | tf_op jit(solution)/shard_map/ppermute | solution.py:19
  213.4 9.9 %collective-permute-done.20 = bf16[128,3072]{1,0:T(8,128)(2,1)S(1)} collective-permute-done((bf16[128,3072]{1,0:T(8,128)(2,1)S(1)}, bf16[128,3072]{1,0:T(8,128)(2,1)S(1)}, u32[]{:S(2)}, u32[]{:S(2)}) %collective-permute-start.20) | collective-permute-done | bytes 786464 | tf_op jit(solution)/shard_map/ppermute | solution.py:19
  248.4 27.8 %conv_gates_scan.1 = (bf16[4,256,768]{2,1,0:T(8,128)(2,1)}, f32[4,256,768]{2,1,0:T(8,128)}, f32[4,256,768]{2,1,0:T(8,128)}, f32[4,256,768]{2,1,0:T(8,128)}, f32[4,256,768]{2,1,0:T(8,128)}) custom-call(bf16[4,256,768]{2,1,0:T(8,128)(2,1)} %bitcast.382, bf16[4,8,768]{2,1,0:T(8,128)(2,1)} %pad.74.edge_ref, f32[4,256,128]{2,1,0:T(8,128)} %pad_convert_fusion.mask_ref, ...), custom_call_target="tpu_custom_call" | custom-call | flops 2415919104 | bytes 15728640 | tf_op jit(solution)/shard_map/conv_gates_scan/pallas_call | solution.py:271
  297.1 21.3 %collective-permute-done.11 = bf16[256,768]{1,0:T(8,128)(2,1)S(1)} collective-permute-done((bf16[256,768]{1,0:T(8,128)(2,1)S(1)}, bf16[256,768]{1,0:T(8,128)(2,1)S(1)}, u32[]{:S(2)}, u32[]{:S(2)}) %collective-permute-start.11) | collective-permute-done | bytes 393248 | tf_op jit(solution)/shard_map/ppermute | solution.py:70
  343.9 8.5 multiply_reduce_fusion
  396.4 36.6 %all-gather.7.cloned.1.call-done = bf16[1024,2048]{1,0:T(8,128)(2,1)} async-done(((bf16[256,2048]{1,0:T(8,128)(2,1)}), bf16[1024,2048]{1,0:T(8,128)(2,1)}) %all-gather.7.cloned.1.call-update) | async-done | bytes 4194320 | tf_op jit(solution)/shard_map/all_gather | solution.py:561
  432.9 19.3 %fusion.114 = f32[1024,3072]{0,1:T(8,128)} fusion(bf16[1024,2048]{1,0:T(8,128)(2,1)} %all-gather.7.cloned.1.call-done, bf16[2048,3072]{1,0:T(8,128)(2,1)} %bitcast.353), kind=kOutput, calls=%fused_computation.362 | convolution fusion | flops 12884901888 | bytes 29360128 | tf_op jit(solution)/shard_map/dot_general | solution.py:145
  452.3 17.9 %fusion.14 = (bf16[1024,1536]{0,1:T(8,128)(2,1)S(1)}, bf16[1024,1536]{0,1:T(8,128)(2,1)}, bf16[1024,1536]{0,1:T(8,128)(2,1)}) fusion(f32[1024,3072]{0,1:T(8,128)} %fusion.114, bf16[2048,1536]{1,0:T(8,128)(2,1)} %bitcast.4, bf16[1024,2048]{1,0:T(8,128)(2,1)S(1)} %bitcast.391), kind=kOutput, calls=%fused_computation.34 | convolution fusion | flops 6480199680 | bytes 32505856 | tf_op jit(solution)/shard_map/dot_general | solution.py:145
  471.8 18.8 %fusion.17 = bf16[1024,2048]{1,0:T(8,128)(2,1)} fusion(bf16[2048,3072]{1,0:T(8,128)(2,1)} %bitcast.354, bf16[1024,1536]{0,1:T(8,128)(2,1)} %get-tuple-element.234, bf16[1024,1536]{0,1:T(8,128)(2,1)S(1)} %get-tuple-element.233), kind=kOutput, calls=%fused_computation.43 | convolution fusion | flops 12899581952 | bytes 23068672 | tf_op jit(solution)/shard_map/dot_general | solution.py:137
  494.5 9.9 %convolution_convert_fusion.2 = bf16[1536,2048]{0,1:T(8,128)(2,1)S(1)} fusion(bf16[1024,1536]{0,1:T(8,128)(2,1)} %get-tuple-element.235, bf16[1024,2048]{1,0:T(8,128)(2,1)} %bitcast.389), kind=kOutput, calls=%fused_computation.22 | convolution fusion | flops 6445596672 | bytes 13631488 | tf_op jit(solution)/shard_map/dot_general | solution.py:141
  508.1 19.5 %convolution_convert_fusion = bf16[2048,3072]{1,0:T(8,128)(2,1)} fusion(bf16[1024,2048]{1,0:T(8,128)(2,1)} %all-gather.7.cloned.1.call-done, bf16[1024,1536]{0,1:T(8,128)(2,1)} %get-tuple-element.234, bf16[1024,1536]{0,1:T(8,128)(2,1)} %copy-done.82), kind=kOutput, calls=%fused_computation.9 | convolution fusion | flops 12903776256 | bytes 23068672 | tf_op jit(solution)/shard_map/dot_general | solution.py:141
  538.9 11.8 %add_convert_fusion = bf16[4,256,2048]{2,1,0:T(8,128)(2,1)} fusion(f32[256,2048]{1,0:T(8,128)S(1)} %get-tuple-element.315, f32[4]{0:T(128)S(1)} %compare_convert_fusion, bf16[4,256,1536]{2,1,0:T(8,128)(2,1)S(1)} %bitcast.378, bf16[2048,1536,1]{1,0,2:T(8,128)(2,1)} %bitcast.49), kind=kOutput, calls=%fused_computation.21 | convolution fusion | flops 6448742400 | bytes 15728656 | tf_op jit(solution)/shard_map/dot_general | solution.py:137
  555.5 13.0 %reduce-scatter.4.cloned.1.call-done = bf16[256,2048]{1,0:T(8,128)(2,1)} async-done(((bf16[1024,2048]{1,0:T(8,128)(2,1)}), bf16[256,2048]{1,0:T(8,128)(2,1)}) %reduce-scatter.4.cloned.1.call-update) | async-done | bytes 1048592 | tf_op jit(solution)/shard_map/reduce_scatter | solution.py:578
  572.3 8.8 convolution_convert_fusion.4
  595.5 14.1 %collective-permute-done.28 = bf16[256,768]{1,0:T(8,128)(2,1)S(1)} collective-permute-done((bf16[256,768]{1,0:T(8,128)(2,1)S(1)}, bf16[256,768]{1,0:T(8,128)(2,1)S(1)}, u32[]{:S(2)}, u32[]{:S(2)}) %collective-permute-start.28) | collective-permute-done | bytes 393248 | tf_op jit(solution)/shard_map/ppermute | solution.py:70
  609.6 8.3 collective-permute-done.29
  619.5 17.5 %reverse_scan.1 = (bf16[4,256,768]{2,1,0:T(8,128)(2,1)}, f32[4,256,768]{2,1,0:T(8,128)}, f32[4,256,768]{2,1,0:T(8,128)}, f32[4,256,768]{2,1,0:T(8,128)}) custom-call(bf16[4,256,768]{2,1,0:T(8,128)(2,1)} %bitcast.370, f32[4,256,768]{2,1,0:T(8,128)} %bitcast.358, f32[4,256,768]{2,1,0:T(8,128)} %get-tuple-element.232.state_ref, ...), custom_call_target="tpu_custom_call" | custom-call | flops 31457280 | bytes 23592960 | tf_op jit(solution)/shard_map/reverse_scan/pallas_call | solution.py:321
  645.5 32.2 %gates_backward.1 = (bf16[4,256,768]{2,1,0:T(8,128)(2,1)}, f32[4,8,768]{2,1,0:T(8,128)}, f32[4,8,768]{2,1,0:T(8,128)}, f32[64,768]{1,0:T(8,128)}, f32[768,1536]{1,0:T(8,128)}) custom-call(f32[4,256,768]{2,1,0:T(8,128)} %get-tuple-element.43.direct_ref, f32[4,256,768]{2,1,0:T(8,128)} %get-tuple-element.44.coef_ref, ...), custom_call_target="tpu_custom_call" | custom-call | flops 4831838208 | bytes 26738688 | tf_op jit(solution)/shard_map/gates_backward/pallas_call | solution.py:432
  683.9 11.4 %fusion.10 = (f32[2048]{0:T(1024)S(1)}, f32[1024]{0:T(1024)S(1)}, f32[1024,2048]{1,0:T(8,128)S(1)}) fusion(bf16[1024,2048]{1,0:T(8,128)(2,1)} %all-gather.5.cloned.1.call-done, f32[1024]{0:T(1024)} %copy-done.71, f32[2048]{0:T(1024)} %bitcast.403, bf16[2048,1536]{1,0:T(8,128)(2,1)} %bitcast.369, bf16[1024,768]{1,0:T(8,128)(2,1)} %bitcast.411, ...), kind=kOutput, calls=%fused_computation.19 | convolution fusion | flops 6463419392 | bytes 22044672 | tf_op jit(solution)/shard_map/dot_general | solution.py:137
  706.7 8.2 fusion
  725.6 27.2 %collective-permute-done.51 = bf16[2,128,3072]{2,1,0:T(8,128)(2,1)} collective-permute-done((bf16[2,128,3072]{2,1,0:T(8,128)(2,1)}, bf16[2,128,3072]{2,1,0:T(8,128)(2,1)}, u32[]{:S(2)}, u32[]{:S(2)}) %collective-permute-start.51) | collective-permute-done | bytes 1572896 | tf_op jit(solution)/shard_map/ppermute | solution.py:19
  775.8 9.4 convolution_convert_fusion.3
  798.6 32.9 %collective-permute-done.61 = f32[4,176,352]{2,1,0:T(8,128)S(1)} collective-permute-done((f32[4,176,352]{2,1,0:T(8,128)S(1)}, f32[4,176,352]{2,1,0:T(8,128)S(1)}, u32[]{:S(2)}, u32[]{:S(2)}) %collective-permute-start.61) | collective-permute-done | bytes 991264 | tf_op jit(solution)/shard_map/ppermute | solution.py:19
  836.1 19.9 %collective-permute-done.36 = f32[10,768]{1,0:T(8,128)S(1)} collective-permute-done((f32[10,768]{1,0:T(8,128)S(1)}, f32[10,768]{1,0:T(8,128)S(1)}, u32[]{:S(2)}, u32[]{:S(2)}) %collective-permute-start.36) | collective-permute-done | bytes 30752 | tf_op jit(solution)/shard_map/ppermute | solution.py:19
  873.9 8.3 collective-permute-done.38
  888.1 27.3 %collective-permute-done.43 = bf16[2,128,3072]{2,1,0:T(8,128)(2,1)S(1)} collective-permute-done((bf16[2,128,3072]{2,1,0:T(8,128)(2,1)S(1)}, bf16[2,128,3072]{2,1,0:T(8,128)(2,1)S(1)}, u32[]{:S(2)}, u32[]{:S(2)}) %collective-permute-start.43) | collective-permute-done | bytes 1572896 | tf_op jit(solution)/shard_map/ppermute | solution.py:19
  917.6 11.8 %collective-permute-done.45 = bf16[2,128,3072]{2,1,0:T(8,128)(2,1)S(1)} collective-permute-done((bf16[2,128,3072]{2,1,0:T(8,128)(2,1)S(1)}, bf16[2,128,3072]{2,1,0:T(8,128)(2,1)S(1)}, u32[]{:S(2)}, u32[]{:S(2)}) %collective-permute-start.45) | collective-permute-done | bytes 1572896 | tf_op jit(solution)/shard_map/ppermute | solution.py:19
  954.1 11.6 %collective-permute-done.49 = bf16[256,768]{1,0:T(8,128)(2,1)} collective-permute-done((bf16[256,768]{1,0:T(8,128)(2,1)}, bf16[256,768]{1,0:T(8,128)(2,1)}, u32[]{:S(2)}, u32[]{:S(2)}) %collective-permute-start.49) | collective-permute-done | bytes 393248 | tf_op jit(solution)/shard_map/ppermute | solution.py:70
  (497 shorter events, 386.0 us)
Async XLA Ops:
  7.2 82.0 %all-gather.5.cloned.1.call-start = ((), (), s32[]{:S(2)}) async-start(), calls=%async_computation.3 | async-start | bytes 5242880 | tf_op jit(solution)/shard_map/all_gather | solution.py:502
  8.0 425.0 %all-gather.7.cloned.1.call-start = ((), (), s32[]{:S(2)}) async-start(), calls=%async_computation.4 | async-start | bytes 5242880 | tf_op jit(solution)/shard_map/all_gather | solution.py:561
  11.3 83.5 %collective-permute-start.5 = (bf16[256,1536]{1,0:T(8,128)(2,1)}, bf16[256,1536]{1,0:T(8,128)(2,1)}, u32[]{:S(2)}, u32[]{:S(2)}) collective-permute-start(bf16[256,1536]{1,0:T(8,128)(2,1)} %fusion.46), channel_id=1, source_target_pairs={{0,8},{4,12},{8,0},{12,4},{1,9},{5,13},{9,1},{13,5},{2,10},{6,14},... | collective-permute-start | bytes 2359304 | tf_op jit(solution)/shard_map/ppermute | solution.py:19
  12.9 86.9 %collective-permute-start.6 = (bf16[256,1536]{1,0:T(8,128)(2,1)}, bf16[256,1536]{1,0:T(8,128)(2,1)}, u32[]{:S(2)}, u32[]{:S(2)}) collective-permute-start(bf16[256,1536]{1,0:T(8,128)(2,1)} %fusion.46), channel_id=1, source_target_pairs={{0,16},{16,0},{1,17},{17,1},{2,18},{18,2},{3,19},{19,3},{4,20},{20... | collective-permute-start | bytes 2359304 | tf_op jit(solution)/shard_map/ppermute | solution.py:19
  94.8 51.9 %collective-permute-start.22 = (bf16[256,3072]{1,0:T(8,128)(2,1)}, bf16[256,3072]{1,0:T(8,128)(2,1)}, u32[]{:S(2)}, u32[]{:S(2)}) collective-permute-start(bf16[256,3072]{1,0:T(8,128)(2,1)} %constant_dynamic-update-slice_fusion.6), channel_id=1, source_target_pairs={{0,8},{4,12},{8,0},{12,4},{1,9},{5,13},{9,1},{13,5},{2,10},{6,14},... | collective-permute-start | bytes 4718600 | tf_op jit(solution)/shard_map/ppermute | solution.py:19
  99.7 52.1 %collective-permute-start.23 = (bf16[256,3072]{1,0:T(8,128)(2,1)}, bf16[256,3072]{1,0:T(8,128)(2,1)}, u32[]{:S(2)}, u32[]{:S(2)}) collective-permute-start(bf16[256,3072]{1,0:T(8,128)(2,1)} %constant_dynamic-update-slice_fusion.6), channel_id=1, source_target_pairs={{0,16},{16,0},{1,17},{17,1},{2,18},{18,2},{3,19},{19,3},{4,20},{20... | collective-permute-start | bytes 4718600 | tf_op jit(solution)/shard_map/ppermute | solution.py:19
  102.3 41.4 %collective-permute-start.7 = (bf16[128,1536]{1,0:T(8,128)(2,1)}, bf16[128,1536]{1,0:T(8,128)(2,1)}, u32[]{:S(2)}, u32[]{:S(2)}) collective-permute-start(bf16[128,1536]{1,0:T(8,128)(2,1)} %slice.394), channel_id=1, source_target_pairs={{0,16},{16,0},{1,17},{17,1},{2,18},{18,2},{3,19},{19,3},{4,20},{20... | collective-permute-start | bytes 1179656 | tf_op jit(solution)/shard_map/ppermute | solution.py:19
  128.0 46.5 %collective-permute-start.17 = (bf16[256,3072]{1,0:T(8,128)(2,1)}, bf16[256,3072]{1,0:T(8,128)(2,1)S(1)}, u32[]{:S(2)}, u32[]{:S(2)}) collective-permute-start(bf16[256,3072]{1,0:T(8,128)(2,1)} %pad_maximum_fusion.15), channel_id=1, source_target_pairs={{0,8},{4,12},{8,0},{12,4},{1,9},{5,13},{9,1},{13,5},{2,10},{6,14},... | collective-permute-start | bytes 4718600 | tf_op jit(solution)/shard_map/ppermute | solution.py:19
  143.7 210.5 %collective-permute-start = (bf16[256,1536]{1,0:T(8,128)(2,1)}, bf16[256,1536]{1,0:T(8,128)(2,1)}, u32[]{:S(2)}, u32[]{:S(2)}) collective-permute-start(bf16[256,1536]{1,0:T(8,128)(2,1)} %bitcast.379), channel_id=1, source_target_pairs={{0,8},{4,12},{8,0},{12,4},{1,9},{5,13},{9,1},{13,5},{2,10},{6,14},... | collective-permute-start | bytes 2359304 | tf_op jit(solution)/shard_map/ppermute | solution.py:19
  145.3 37.6 %collective-permute-start.18 = (bf16[256,3072]{1,0:T(8,128)(2,1)}, bf16[256,3072]{1,0:T(8,128)(2,1)S(1)}, u32[]{:S(2)}, u32[]{:S(2)}) collective-permute-start(bf16[256,3072]{1,0:T(8,128)(2,1)} %pad_maximum_fusion.15), channel_id=1, source_target_pairs={{0,16},{16,0},{1,17},{17,1},{2,18},{18,2},{3,19},{19,3},{4,20},{20... | collective-permute-start | bytes 4718600 | tf_op jit(solution)/shard_map/ppermute | solution.py:19
  147.9 51.9 %collective-permute-start.24 = (bf16[128,3072]{1,0:T(8,128)(2,1)S(1)}, bf16[128,3072]{1,0:T(8,128)(2,1)S(1)}, u32[]{:S(2)}, u32[]{:S(2)}) collective-permute-start(bf16[128,3072]{1,0:T(8,128)(2,1)S(1)} %slice.408), channel_id=1, source_target_pairs={{0,16},{16,0},{1,17},{17,1},{2,18},{18,2},{3,19},{19,3},{4,20},{20... | collective-permute-start | bytes 2359304 | tf_op jit(solution)/shard_map/ppermute | solution.py:19
  153.1 55.2 %collective-permute-start.25 = (bf16[128,3072]{1,0:T(8,128)(2,1)S(1)}, bf16[128,3072]{1,0:T(8,128)(2,1)S(1)}, u32[]{:S(2)}, u32[]{:S(2)}) collective-permute-start(bf16[128,3072]{1,0:T(8,128)(2,1)S(1)} %slice.409), channel_id=1, source_target_pairs={{0,8},{4,12},{8,0},{12,4},{1,9},{5,13},{9,1},{13,5},{2,10},{6,14},... | collective-permute-start | bytes 2359304 | tf_op jit(solution)/shard_map/ppermute | solution.py:19
  174.6 38.7 %collective-permute-start.19 = (bf16[128,3072]{1,0:T(8,128)(2,1)S(1)}, bf16[128,3072]{1,0:T(8,128)(2,1)S(1)}, u32[]{:S(2)}, u32[]{:S(2)}) collective-permute-start(bf16[128,3072]{1,0:T(8,128)(2,1)S(1)} %slice.405), channel_id=1, source_target_pairs={{0,16},{16,0},{1,17},{17,1},{2,18},{18,2},{3,19},{19,3},{4,20},{20... | collective-permute-start | bytes 2359304 | tf_op jit(solution)/shard_map/ppermute | solution.py:19
  182.9 50.8 %collective-permute-start.9 = (bf16[4,1,256,1536]{3,2,0,1:T(8,128)(2,1)S(1)}, bf16[4,1,256,1536]{3,2,0,1:T(8,128)(2,1)S(1)}, u32[]{:S(2)}, u32[]{:S(2)}) collective-permute-start(bf16[4,1,256,1536]{3,2,0,1:T(8,128)(2,1)S(1)} %bitcast.360), channel_id=1, source_target_pairs={{0,4},{4,0},{8,12},{12,8},{1,5},{5,1},{9,13},{13,9},{2,6},{6,2},{1... | collective-permute-start | bytes 9437192 | tf_op jit(solution)/shard_map/ppermute | solution.py:19
  228.9 109.2 %collective-permute-start.21 = (bf16[4,1,256,3072]{3,2,1,0:T(8,128)(2,1)}, bf16[4,1,256,3072]{3,2,1,0:T(8,128)(2,1)}, u32[]{:S(2)}, u32[]{:S(2)}) collective-permute-start(bf16[4,1,256,3072]{3,2,1,0:T(8,128)(2,1)} %bitcast.40), channel_id=1, source_target_pairs={{0,4},{4,0},{8,12},{12,8},{1,5},{5,1},{9,13},{13,9},{2,6},{6,2},{1... | collective-permute-start | bytes 18874376 | tf_op jit(solution)/shard_map/ppermute | solution.py:19
  318.4 72.1 %collective-permute-start.26 = (bf16[4,1,256,3072]{3,2,1,0:T(8,128)(2,1)}, bf16[4,1,256,3072]{3,2,1,0:T(8,128)(2,1)}, u32[]{:S(2)}, u32[]{:S(2)}) collective-permute-start(bf16[4,1,256,3072]{3,2,1,0:T(8,128)(2,1)} %bitcast.45), channel_id=1, source_target_pairs={{0,4},{4,0},{8,12},{12,8},{1,5},{5,1},{9,13},{13,9},{2,6},{6,2},{1... | collective-permute-start | bytes 18874376 | tf_op jit(solution)/shard_map/ppermute | solution.py:19
  353.7 214.8 %reduce-scatter.4.cloned.1.call-start = ((), (), s32[]{:S(2)}) async-start(), calls=%async_computation.5 | async-start | bytes 5242880 | tf_op jit(solution)/shard_map/reduce_scatter | solution.py:578
  490.6 460.7 %reduce-scatter.8.cloned.1.call-start = ((), (), s32[]{:S(2)}) async-start(), calls=%async_computation.7 | async-start | bytes 5242880 | tf_op jit(solution)/shard_map/reduce_scatter | solution.py:627
  508.1 42.6 %collective-permute-start.55 = (bf16[4,256,1536]{2,1,0:T(8,128)(2,1)}, bf16[4,256,1536]{2,1,0:T(8,128)(2,1)}, u32[]{:S(2)}, u32[]{:S(2)}) collective-permute-start(bf16[4,256,1536]{2,1,0:T(8,128)(2,1)} %dynamic-slice_bitcast_fusion.2), channel_id=1, source_target_pairs={{0,4},{4,0},{8,12},{12,8},{1,5},{5,1},{9,13},{13,9},{2,6},{6,2},{1... | collective-permute-start | bytes 9437192 | tf_op jit(solution)/shard_map/ppermute | solution.py:19
  538.3 168.4 %collective-permute-start.50 = (bf16[4,256,3072]{2,1,0:T(8,128)(2,1)}, bf16[4,256,3072]{2,1,0:T(8,128)(2,1)}, u32[]{:S(2)}, u32[]{:S(2)}) collective-permute-start(bf16[4,256,3072]{2,1,0:T(8,128)(2,1)} %dynamic-slice_bitcast_fusion), channel_id=1, source_target_pairs={{0,4},{4,0},{8,12},{12,8},{1,5},{5,1},{9,13},{13,9},{2,6},{6,2},{1... | collective-permute-start | bytes 18874376 | tf_op jit(solution)/shard_map/ppermute | solution.py:19
  587.1 92.8 %collective-permute-start.56 = (bf16[2,128,1536]{2,1,0:T(8,128)(2,1)}, bf16[2,128,1536]{2,1,0:T(8,128)(2,1)}, u32[]{:S(2)}, u32[]{:S(2)}) collective-permute-start(bf16[2,128,1536]{2,1,0:T(8,128)(2,1)} %dynamic-slice_bitcast_fusion.9), channel_id=1, source_target_pairs={{0,16},{16,0},{1,17},{17,1},{2,18},{18,2},{3,19},{19,3},{4,20},{20... | collective-permute-start | bytes 2359304 | tf_op jit(solution)/shard_map/ppermute | solution.py:19
  594.0 110.0 %collective-permute-start.58 = (bf16[2,128,1536]{2,1,0:T(8,128)(2,1)}, bf16[2,128,1536]{2,1,0:T(8,128)(2,1)}, u32[]{:S(2)}, u32[]{:S(2)}) collective-permute-start(bf16[2,128,1536]{2,1,0:T(8,128)(2,1)} %dynamic-slice_bitcast_fusion.8), channel_id=1, source_target_pairs={{0,8},{4,12},{8,0},{12,4},{1,9},{5,13},{9,1},{13,5},{2,10},{6,14},... | collective-permute-start | bytes 2359304 | tf_op jit(solution)/shard_map/ppermute | solution.py:19
  699.5 273.2 %reduce-scatter.6.cloned.1.call-start = ((), (), s32[]{:S(2)}) async-start(), calls=%async_computation.6 | async-start | bytes 5242880 | tf_op jit(solution)/shard_map/reduce_scatter | solution.py:581
  754.9 38.2 %collective-permute-start.52 = (bf16[128,3072]{1,0:T(8,128)(2,1)S(1)}, bf16[128,3072]{1,0:T(8,128)(2,1)}, u32[]{:S(2)}, u32[]{:S(2)}) collective-permute-start(bf16[128,3072]{1,0:T(8,128)(2,1)S(1)} %dynamic-slice_bitcast_fusion.11), channel_id=1, source_target_pairs={{0,8},{4,12},{8,0},{12,4},{1,9},{5,13},{9,1},{13,5},{2,10},{6,14},... | collective-permute-start | bytes 2359304 | tf_op jit(solution)/shard_map/ppermute | solution.py:19
  771.5 93.2 %collective-permute-start.42 = (bf16[4,256,3072]{2,1,0:T(8,128)(2,1)}, bf16[4,256,3072]{2,1,0:T(8,128)(2,1)}, u32[]{:S(2)}, u32[]{:S(2)}) collective-permute-start(bf16[4,256,3072]{2,1,0:T(8,128)(2,1)} %dynamic-slice_bitcast_fusion.1), channel_id=1, source_target_pairs={{0,4},{4,0},{8,12},{12,8},{1,5},{5,1},{9,13},{13,9},{2,6},{6,2},{1... | collective-permute-start | bytes 18874376 | tf_op jit(solution)/shard_map/ppermute | solution.py:19
  789.7 43.5 %collective-permute-start.54 = (bf16[128,3072]{1,0:T(8,128)(2,1)S(1)}, bf16[128,3072]{1,0:T(8,128)(2,1)S(1)}, u32[]{:S(2)}, u32[]{:S(2)}) collective-permute-start(bf16[128,3072]{1,0:T(8,128)(2,1)S(1)} %dynamic-slice_bitcast_fusion.10), channel_id=1, source_target_pairs={{0,16},{16,0},{1,17},{17,1},{2,18},{18,2},{3,19},{19,3},{4,20},{20... | collective-permute-start | bytes 2359304 | tf_op jit(solution)/shard_map/ppermute | solution.py:19
  791.7 67.6 %collective-permute-start.37 = (bf16[4,256,1536]{2,1,0:T(8,128)(2,1)S(1)}, bf16[4,256,1536]{2,1,0:T(8,128)(2,1)S(1)}, u32[]{:S(2)}, u32[]{:S(2)}) collective-permute-start(bf16[4,256,1536]{2,1,0:T(8,128)(2,1)S(1)} %dynamic-slice_bitcast_fusion.3), channel_id=1, source_target_pairs={{0,4},{4,0},{8,12},{12,8},{1,5},{5,1},{9,13},{13,9},{2,6},{6,2},{1... | collective-permute-start | bytes 9437192 | tf_op jit(solution)/shard_map/ppermute | solution.py:19
  792.0 39.5 %collective-permute-start.61 = (f32[4,176,352]{2,1,0:T(8,128)S(1)}, f32[4,176,352]{2,1,0:T(8,128)S(1)}, u32[]{:S(2)}, u32[]{:S(2)}) collective-permute-start(f32[4,176,352]{2,1,0:T(8,128)S(1)} %fusion.128), channel_id=1, source_target_pairs={{0,16},{16,0},{1,17},{17,1},{2,18},{18,2},{3,19},{19,3},{4,20},{20... | collective-permute-start | bytes 2973704 | tf_op jit(solution)/shard_map/ppermute | solution.py:19
  872.8 42.7 %collective-permute-start.43 = (bf16[2,128,3072]{2,1,0:T(8,128)(2,1)S(1)}, bf16[2,128,3072]{2,1,0:T(8,128)(2,1)S(1)}, u32[]{:S(2)}, u32[]{:S(2)}) collective-permute-start(bf16[2,128,3072]{2,1,0:T(8,128)(2,1)S(1)} %dynamic-slice_bitcast_fusion.7), channel_id=1, source_target_pairs={{0,16},{16,0},{1,17},{17,1},{2,18},{18,2},{3,19},{19,3},{4,20},{20... | collective-permute-start | bytes 4718600 | tf_op jit(solution)/shard_map/ppermute | solution.py:19
  883.6 47.4 %collective-permute-start.39 = (bf16[128,1536]{1,0:T(8,128)(2,1)S(1)}, bf16[128,1536]{1,0:T(8,128)(2,1)S(1)}, u32[]{:S(2)}, u32[]{:S(2)}) collective-permute-start(bf16[128,1536]{1,0:T(8,128)(2,1)S(1)} %dynamic-slice_bitcast_fusion.19), channel_id=1, source_target_pairs={{0,8},{4,12},{8,0},{12,4},{1,9},{5,13},{9,1},{13,5},{2,10},{6,14},... | collective-permute-start | bytes 1179656 | tf_op jit(solution)/shard_map/ppermute | solution.py:19
  885.2 44.3 %collective-permute-start.45 = (bf16[2,128,3072]{2,1,0:T(8,128)(2,1)S(1)}, bf16[2,128,3072]{2,1,0:T(8,128)(2,1)S(1)}, u32[]{:S(2)}, u32[]{:S(2)}) collective-permute-start(bf16[2,128,3072]{2,1,0:T(8,128)(2,1)S(1)} %dynamic-slice_bitcast_fusion.6), channel_id=1, source_target_pairs={{0,8},{4,12},{8,0},{12,4},{1,9},{5,13},{9,1},{13,5},{2,10},{6,14},... | collective-permute-start | bytes 4718600 | tf_op jit(solution)/shard_map/ppermute | solution.py:19
  887.2 59.5 %collective-permute-start.41 = (bf16[128,1536]{1,0:T(8,128)(2,1)S(1)}, bf16[128,1536]{1,0:T(8,128)(2,1)S(1)}, u32[]{:S(2)}, u32[]{:S(2)}) collective-permute-start(bf16[128,1536]{1,0:T(8,128)(2,1)S(1)} %dynamic-slice_bitcast_fusion.18), channel_id=1, source_target_pairs={{0,16},{16,0},{1,17},{17,1},{2,18},{18,2},{3,19},{19,3},{4,20},{20... | collective-permute-start | bytes 1179656 | tf_op jit(solution)/shard_map/ppermute | solution.py:19
  (121 other events, 2319.1 us)
Sparse Core Ops, SparseCore 0:
  9.6 79.5 all-gather.4
  353.9 79.0 all-gather.6
  490.8 77.7 reduce-scatter.3
  699.7 78.8 reduce-scatter.7
  781.3 77.3 reduce-scatter.5
